TPU v7x, 32 devices: a whole 2x2x4 slice. The times are simulated.
32 devices in a mesh: grp: 2 (over y), gen: 4 (over z), row: 2 (over x), ch: 2 (over core).
Axes of the slice: x: 2, y: 2, z: 4, core: 2. Of those that a mesh axis runs over, the one named last changes fastest.
Arguments:
- x_center: bfloat16 [24, 24, 112], P(('grp', 'row')), parts along dimension 0, may hold values from -6 to 6
- x_gens: bfloat16 [256, 12, 24, 112], P(('grp', 'gen'), 'row'), parts along dimension 0, may hold values from -0.125 to 0.125
- w_expand: bfloat16 [112, 672], P(None, 'ch'), may hold values from -0.5 to 0.5
- b_expand: float32 [672], P('ch'), may hold values from -3 to 3
- w_depth: float32 [5, 5, 672], P(None, None, 'ch'), may hold values from -1.25 to 1.25
- b_depth: float32 [672], P('ch'), may hold values from -3 to 3
- w_reduce: float32 [672, 28], replicated, may hold values from -0.25 to 0.25
- b_reduce: float32 [28], replicated, may hold values from -6 to 6
- w_excite: float32 [28, 672], P(None, 'ch'), may hold values from -1 to 1
- b_excite: float32 [672], P('ch'), may hold values from -3 to 3
Outputs:
- out_center: float32 [24, 24, 672], P(('grp', 'row'), None, 'ch'), parts along dimension 0
- out_gens: bfloat16 [256, 12, 24, 672], P(('grp', 'gen'), 'row', None, 'ch'), parts along dimension 0
- out_box: float32 [24, 24, 672], P(('grp', 'row'), None, 'ch'), parts along dimension 0
There are 2 independent parts, one for each index of `grp`. A program takes and returns all parts, laid end to end along the dimension named above; an argument that names none is the same for every part. Nothing has to cross between parts.
All inputs are finite; a program needn't handle non-finite values.
Results may differ from a plain program's by a relative error of at most 0.007.
Values may be sent and summed in bfloat16 or wider, within the bound.
A program may use at most 64 MiB of HBM per device.

v0:
```python
import jax
import jax.numpy as jnp
from jax import lax
from jax.sharding import PartitionSpec as P


def padded_2(cells, sides, width):
    for axis, dim in sides:
        count = lax.axis_size(axis)
        ends = count - 1
        head = lax.slice_in_dim(cells, 0, width, axis=dim)
        tail = lax.slice_in_dim(cells, cells.shape[dim] - width, cells.shape[dim], axis=dim)
        cells = jnp.concatenate(
            [
                lax.ppermute(tail, axis, [(i, (i + 1) % count) for i in range(ends)]),
                cells,
                lax.ppermute(head, axis, [((i + 1) % count, i) for i in range(ends)]),
            ],
            axis=dim,
        )
    return cells


def depthwise(padded, w_depth, row_count, col_count):
    accum_sum = jnp.zeros(padded.shape[:-3] + (row_count, col_count, padded.shape[-1]), jnp.float32)
    for tap_row in range(w_depth.shape[0]):
        for tap_col in range(w_depth.shape[1]):
            window = padded[..., tap_row : tap_row + row_count, tap_col : tap_col + col_count, :]
            accum_sum = accum_sum + window.astype(jnp.float32) * w_depth[tap_row, tap_col]
    return accum_sum


def relax_gate(ex_center, gate_radius):
    low_end = ex_center - gate_radius
    high_end = ex_center + gate_radius
    sig_low = jax.nn.sigmoid(low_end)
    sig_high = jax.nn.sigmoid(high_end)
    slope_val = jnp.minimum(sig_low * (1.0 - sig_low), sig_high * (1.0 - sig_high))
    gate_center = slope_val * ex_center + 0.5 * (
        sig_high + sig_low - slope_val * (high_end + low_end)
    )
    spread_term = 0.5 * (sig_high - sig_low - slope_val * (high_end - low_end))
    return (gate_center, slope_val, spread_term)


def on_device(
    x_center, x_gens, w_expand, b_expand, w_depth, b_depth, w_reduce, b_reduce, w_excite, b_excite
):
    precise = lax.Precision.HIGHEST
    row_count = x_center.shape[0]
    col_count = x_center.shape[1]
    margin = w_depth.shape[0] // 2
    height = row_count * lax.axis_size("row")
    own_center = (
        jnp.dot(x_center, w_expand, preferred_element_type=jnp.float32) + b_expand
    ).astype(jnp.bfloat16)
    own_gens = jnp.dot(x_gens, w_expand, preferred_element_type=jnp.float32).astype(jnp.bfloat16)
    padded_center, exp_gens = (
        padded_2(own_center[None], (("row", 1),), margin),
        padded_2(own_gens, (("row", 1),), margin),
    )
    exp_center = padded_center[0]
    dw_center = (
        depthwise(
            jnp.pad(exp_center, ((0, 0), (margin, margin), (0, 0))), w_depth, row_count, col_count
        )
        + b_depth
    )
    dw_gens = depthwise(
        jnp.pad(exp_gens, ((0, 0), (0, 0), (margin, margin), (0, 0))), w_depth, row_count, col_count
    ).astype(jnp.bfloat16)
    local_radius = jnp.sum(jnp.abs(dw_gens).astype(jnp.float32), axis=0)
    feat_radius = lax.psum(local_radius.astype(jnp.bfloat16), "gen").astype(jnp.float32)
    inv_cells = 1.0 / (height * col_count)
    pool_center = jnp.sum(dw_center, axis=(0, 1)) * inv_cells
    pool_gens = jnp.sum(dw_gens.astype(jnp.float32), axis=(1, 2)) * inv_cells
    pool_center, pool_gens = lax.psum((pool_center, pool_gens), "row")
    pool_center, pool_gens = (
        lax.all_gather(pool_center, "ch", axis=0, tiled=True),
        lax.all_gather(pool_gens, "ch", axis=1, tiled=True),
    )
    sq_center = jnp.dot(pool_center, w_reduce, precision=precise) + b_reduce
    sq_gens = jnp.dot(pool_gens, w_reduce, precision=precise)
    ex_center = jnp.dot(sq_center, w_excite, precision=precise) + b_excite
    ex_gens = jnp.dot(sq_gens, w_excite, precision=precise)
    local_gate = jnp.sum(jnp.abs(ex_gens), axis=0)
    gate_radius = lax.psum(local_gate, "gen")
    gate_center, slope_val, spread_term = relax_gate(ex_center, gate_radius)
    gate_gens = slope_val * ex_gens
    gate_total = slope_val * gate_radius + spread_term
    out_center = dw_center * gate_center
    out_gens = (
        dw_center[None] * gate_gens[:, None, None, :] + gate_center * dw_gens.astype(jnp.float32)
    ).astype(jnp.bfloat16)
    out_box = jnp.abs(dw_center) * spread_term + feat_radius * gate_total
    return (out_center, out_gens, out_box)


def solution(mesh):
    in_specs = (
        P(("grp", "row"), None, None),
        P(("grp", "gen"), "row", None, None),
        P(None, "ch"),
        P("ch"),
        P(None, None, "ch"),
        P("ch"),
        P(),
        P(),
        P(None, "ch"),
        P("ch"),
    )
    out_specs = (
        P(("grp", "row"), None, "ch"),
        P(("grp", "gen"), "row", None, "ch"),
        P(("grp", "row"), None, "ch"),
    )
    return jax.shard_map(
        on_device, mesh=mesh, in_specs=in_specs, out_specs=out_specs, check_vma=False
    )
```

profile of v0, /device:TPU:0, one launch (start us, length us, event | category | flops | bytes accessed | tf_op | source)
XLA Modules:
  0.0 158.3 jit_solution(7868067441693738180)
XLA Ops:
  7.2 0.0 copy-start
  7.2 0.0 copy-start.30
  7.2 0.0 copy-start.7
  7.2 0.0 copy-start.8
  7.2 0.0 copy-start.28
  7.2 0.0 copy-start.9
  7.2 0.0 all-reduce.6.cloned.1.call-start
  7.3 1.3 copy-done
  8.5 2.3 %convolution_convert_fusion = bf16[32,6,24,336]{3,2,1,0:T(8,128)(2,1)S(1)} fusion(bf16[32,6,24,112]{3,2,1,0:T(8,128)(2,1)S(1)} %copy-done, bf16[112,336]{1,0:T(8,128)(2,1)} %param.12), kind=kOutput, calls=%fused_computation.22 | convolution fusion | flops 348364800 | bytes 4204032 | tf_op jit(solution)/shard_map/dot_general | solution.py:57
  10.8 0.0 copy-start.1
  10.8 1.8 %copy-done.1 = bf16[32,6,24,336]{3,2,1,0:T(8,128)(2,1)} copy-done((bf16[32,6,24,336]{3,2,1,0:T(8,128)(2,1)}, bf16[32,6,24,336]{3,2,1,0:T(8,128)(2,1)S(1)}, u32[]{:S(2)}) %copy-start.1) | copy-done | bytes 3096600
  12.6 1.6 %fusion.48 = (bf16[32,2,24,336]{3,2,1,0:T(8,128)(2,1)}, bf16[32,2,24,336]{3,2,1,0:T(8,128)(2,1)}) fusion(bf16[32,6,24,336]{3,2,1,0:T(8,128)(2,1)S(1)} %convolution_convert_fusion), kind=kLoop, calls=%fused_computation.132 | loop fusion | bytes 4128768 | tf_op jit(solution)/shard_map/slice | solution.py:12
  14.3 4.9 %collective-permute-start.2 = (bf16[32,2,24,336]{3,2,1,0:T(8,128)(2,1)}, bf16[32,2,24,336]{3,2,1,0:T(8,128)(2,1)S(1)}, u32[]{:S(2)}, u32[]{:S(2)}) collective-permute-start(bf16[32,2,24,336]{3,2,1,0:T(8,128)(2,1)} %get-tuple-element.36), channel_id=1, source_target_pairs={{0,2},{1,3},{4,6},{5,7},{8,10},{9,11},{12,14},{13,15},{16,18},{17,... | collective-permute-start | bytes 3096584 | tf_op jit(solution)/shard_map/ppermute | solution.py:15
  19.2 1.3 collective-permute-start.3
  20.5 0.2 fusion.10
  20.7 5.6 %collective-permute-start = (bf16[1,2,24,336]{3,2,1,0:T(8,128)(2,1)S(1)}, bf16[1,2,24,336]{3,2,1,0:T(8,128)(2,1)S(1)}, u32[]{:S(2)}, u32[]{:S(2)}) collective-permute-start(bf16[1,2,24,336]{3,2,1,0:T(8,128)(2,1)S(1)} %get-tuple-element.40), channel_id=1, source_target_pairs={{0,2},{1,3},{4,6},{5,7},{8,10},{9,11},{12,14},{13,15},{16,18},{17,... | collective-permute-start | bytes 96776 | tf_op jit(solution)/shard_map/ppermute | solution.py:15
  26.3 1.3 collective-permute-start.1
  27.6 0.1 slice_reduce_fusion.24
  27.9 0.6 dynamic-slice
  29.2 16.1 %collective-permute-done = bf16[1,2,24,336]{3,2,1,0:T(8,128)(2,1)S(1)} collective-permute-done((bf16[1,2,24,336]{3,2,1,0:T(8,128)(2,1)S(1)}, bf16[1,2,24,336]{3,2,1,0:T(8,128)(2,1)S(1)}, u32[]{:S(2)}, u32[]{:S(2)}) %collective-permute-start) | collective-permute-done | bytes 32288 | tf_op jit(solution)/shard_map/ppermute | solution.py:15
  45.3 4.2 %collective-permute-done.1 = bf16[1,2,24,336]{3,2,1,0:T(8,128)(2,1)S(1)} collective-permute-done((bf16[1,2,24,336]{3,2,1,0:T(8,128)(2,1)S(1)}, bf16[1,2,24,336]{3,2,1,0:T(8,128)(2,1)S(1)}, u32[]{:S(2)}, u32[]{:S(2)}) %collective-permute-start.1) | collective-permute-done | bytes 32288 | tf_op jit(solution)/shard_map/ppermute | solution.py:17
  49.5 0.0 copy-start.2
  49.6 1.3 fusion.46
  50.9 0.6 broadcast_multiply_fusion.3
  51.5 0.0 collective-permute-done.2
  51.7 1.0 copy-done.4
  52.7 0.0 collective-permute-done.3
  52.7 5.7 %fusion.5 = bf16[32,10,28,336]{3,2,1,0:T(8,128)(2,1)S(1)} fusion(bf16[32,2,24,336]{3,2,1,0:T(8,128)(2,1)} %collective-permute-done.3, bf16[32,6,24,336]{3,2,1,0:T(8,128)(2,1)} %copy-done.1, bf16[32,2,24,336]{3,2,1,0:T(8,128)(2,1)} %copy-done.4), kind=kLoop, calls=%fused_computation.9 | loop fusion | flops 36126720 | bytes 11182080 | tf_op jit(solution)/shard_map/concatenate | solution.py:13
  58.4 0.0 copy-start.6
  58.5 27.4 %abs_reduce_fusion = (bf16[6,24,336]{2,1,0:T(8,128)(2,1)}, bf16[32,6,24,336]{3,2,1,0:T(8,128)(2,1)S(1)}) fusion(f32[336]{0:T(512)} %copy-done.26, bf16[32,10,28,336]{3,2,1,0:T(8,128)(2,1)S(1)} %fusion.5, f32[336]{0:T(512)} %copy-done.27, f32[336]{0:T(512)S(1)} %get-tuple-element.4, bf16[32,2,24,336]{3,2,1,0:T(8,128)(2,1)} %collective-permute-done.3, ...), kind=kLoop, calls=%fused_computation.21 | loop fusion | flops 125362944 | bytes 70319424 | tf_op jit(solution)/shard_map/reduce_sum | solution.py:72
  85.9 1.8 %copy-done.3 = bf16[32,6,24,336]{3,2,1,0:T(8,128)(2,1)} copy-done((bf16[32,6,24,336]{3,2,1,0:T(8,128)(2,1)}, bf16[32,6,24,336]{3,2,1,0:T(8,128)(2,1)S(1)}, u32[]{:S(2)}) %copy-start.3) | copy-done | bytes 3096600
  87.7 0.6 convert_reduce_fusion
  88.3 7.8 %all-reduce.3 = (f32[336]{0:T(512)S(1)}, f32[32,336]{1,0:T(8,128)S(1)}) all-reduce(f32[336]{0:T(512)} %broadcast_multiply_fusion.3, f32[32,336]{1,0:T(8,128)S(1)} %broadcast_multiply_fusion.2), channel_id=1, replica_groups=mesh['grp'=2,'gen'=4,'row'=2,'ch'=2] {'row'}, use_global_device_ids=true, to_apply=%region_1.2 | all-reduce | flops 11088 | bytes 88704 | tf_op jit(solution)/shard_map/psum | solution.py:77
  96.1 1.9 %all-gather = f32[2,336,32]{1,2,0:T(8,128)S(1)} all-gather(f32[1,336,32]{1,2,0:T(8,128)S(1)} %bitcast.62), channel_id=1, replica_groups=mesh['grp'=2,'gen'=4,'row'=2,'ch'=2] {'ch'}, dimensions={0}, use_global_device_ids=true | all-gather | bytes 129024 | tf_op jit(solution)/shard_map/all_gather | solution.py:80
  98.0 0.1 copy.13
  98.1 0.1 reshape.62
  98.2 0.2 fusion.50
  98.4 1.0 abs_reduce_fusion.1
  99.4 12.0 %psum.30 = f32[336]{0:T(512)S(1)} all-reduce(f32[336]{0:T(512)S(1)} %get-tuple-element.45), channel_id=1, replica_groups=mesh['grp'=2,'gen'=4,'row'=2,'ch'=2] {'gen'}, use_global_device_ids=true, to_apply=%region_5.6 | all-reduce | flops 336 | bytes 2688 | tf_op jit(solution)/shard_map/psum | solution.py:87
  111.4 0.2 dynamic-update-slice
  111.6 2.4 %all-reduce.2 = f32[672]{0:T(1024)S(1)} all-reduce(f32[672]{0:T(1024)S(1)} %dynamic-update-slice), channel_id=1, replica_groups=mesh['grp'=2,'gen'=4,'row'=2,'ch'=2] {'ch'}, use_global_device_ids=true, to_apply=%add.2 | all-reduce | flops 672 | bytes 5376
  114.1 0.8 fusion.12
  114.9 1.0 convolution_reduce_fusion
  115.9 0.7 subtract_multiply_fusion.2
  116.6 0.0 all-reduce.6.cloned.1.call-update
  116.7 5.0 %fusion.7 = bf16[32,6,24,336]{3,2,1,0:T(8,128)(2,1)} fusion(bf16[32,6,24,336]{3,2,1,0:T(8,128)(2,1)} %copy-done.3, f32[336]{0:T(512)S(1)} %get-tuple-element.43, f32[32,336]{1,0:T(8,128)S(1)} %broadcast_multiply_fusion.1, f32[6,24,336]{2,1,0:T(8,128)} %get-tuple-element.35), kind=kLoop, calls=%fused_computation.11 | loop fusion | flops 7741440 | bytes 6431040 | tf_op jit(solution)/shard_map/convert_element_type | solution.py:94
  121.7 28.1 %all-reduce.6.cloned.1.call-done = bf16[6,24,336]{2,1,0:T(8,128)(2,1)} async-done(((bf16[6,24,336]{2,1,0:T(8,128)(2,1)}), bf16[6,24,336]{2,1,0:T(8,128)(2,1)}) %all-reduce.6.cloned.1.call-update) | async-done | bytes 96784 | tf_op jit(solution)/shard_map/psum | solution.py:73
  149.7 1.7 %multiply_add_fusion = (f32[6,24,336]{2,1,0:T(8,128)}, f32[6,24,336]{2,1,0:T(8,128)}) fusion(bf16[6,24,336]{2,1,0:T(8,128)(2,1)} %all-reduce.6.cloned.1.call-done, f32[6,24,336]{2,1,0:T(8,128)S(1)} %copy-done.5, f32[336]{0:T(512)S(1)} %get-tuple-element.42, f32[336]{0:T(512)S(1)} %get-tuple-element.30, f32[336]{0:T(512)S(1)} %get-tuple-element.43), kind=kLoop, calls=%fused_computation.77 | loop fusion | flops 290304 | bytes 681408 | tf_op jit(solution)/shard_map/add | solution.py:95
  (57 shorter events, 0.3 us)
Async XLA Ops:
  7.2 1.4 copy-start
  7.2 20.7 %copy-start.30 = (u32[32]{0:T(128)S(1)}, u32[32]{0:T(128)}, u32[]{:S(2)}) copy-start(u32[32]{0:T(128)} %constant.20) | copy-start | bytes 388
  7.2 13.3 %copy-start.7 = (bf16[112,336]{1,0:T(8,128)(2,1)S(1)}, bf16[112,336]{1,0:T(8,128)(2,1)}, u32[]{:S(2)}) copy-start(bf16[112,336]{1,0:T(8,128)(2,1)} %param.12) | copy-start | bytes 225796
  7.2 13.3 %copy-start.8 = (bf16[6,24,112]{2,1,0:T(8,128)(2,1)S(1)}, bf16[6,24,112]{2,1,0:T(8,128)(2,1)}, u32[]{:S(2)}) copy-start(bf16[6,24,112]{2,1,0:T(8,128)(2,1)} %param.10) | copy-start | bytes 96772
  7.2 13.3 %copy-start.28 = (f32[336]{0:T(512)S(1)}, f32[336]{0:T(512)}, u32[]{:S(2)}) copy-start(f32[336]{0:T(512)} %param.13) | copy-start | bytes 4036
  7.2 20.4 %copy-start.9 = (f32[5,5,336]{2,1,0:T(8,128)S(1)}, f32[5,5,336]{2,1,0:T(8,128)}, u32[]{:S(2)}) copy-start(f32[5,5,336]{2,1,0:T(8,128)} %param.14) | copy-start | bytes 100804
  7.2 42.3 %copy-start.29 = (f32[336]{0:T(512)S(1)}, f32[336]{0:T(512)}, u32[]{:S(2)}) copy-start(f32[336]{0:T(512)} %param.15) | copy-start | bytes 4036
  7.2 142.5 %all-reduce.6.cloned.1.call-start = ((), (), s32[]{:S(2)}) async-start(), calls=%async_computation | async-start | bytes 221184 | tf_op jit(solution)/shard_map/psum | solution.py:73
  10.8 1.8 %copy-start.1 = (bf16[32,6,24,336]{3,2,1,0:T(8,128)(2,1)}, bf16[32,6,24,336]{3,2,1,0:T(8,128)(2,1)S(1)}, u32[]{:S(2)}) copy-start(bf16[32,6,24,336]{3,2,1,0:T(8,128)(2,1)S(1)} %convolution_convert_fusion) | copy-start | bytes 9289732
  14.3 37.2 %collective-permute-start.2 = (bf16[32,2,24,336]{3,2,1,0:T(8,128)(2,1)}, bf16[32,2,24,336]{3,2,1,0:T(8,128)(2,1)S(1)}, u32[]{:S(2)}, u32[]{:S(2)}) collective-permute-start(bf16[32,2,24,336]{3,2,1,0:T(8,128)(2,1)} %get-tuple-element.36), channel_id=1, source_target_pairs={{0,2},{1,3},{4,6},{5,7},{8,10},{9,11},{12,14},{13,15},{16,18},{17,... | collective-permute-start | bytes 3096584 | tf_op jit(solution)/shard_map/ppermute | solution.py:15
  19.2 33.5 %collective-permute-start.3 = (bf16[32,2,24,336]{3,2,1,0:T(8,128)(2,1)}, bf16[32,2,24,336]{3,2,1,0:T(8,128)(2,1)}, u32[]{:S(2)}, u32[]{:S(2)}) collective-permute-start(bf16[32,2,24,336]{3,2,1,0:T(8,128)(2,1)} %get-tuple-element.37), channel_id=1, source_target_pairs={{2,0},{3,1},{6,4},{7,5},{10,8},{11,9},{14,12},{15,13},{18,16},{19,... | collective-permute-start | bytes 3096584 | tf_op jit(solution)/shard_map/ppermute | solution.py:17
  20.7 24.6 %collective-permute-start = (bf16[1,2,24,336]{3,2,1,0:T(8,128)(2,1)S(1)}, bf16[1,2,24,336]{3,2,1,0:T(8,128)(2,1)S(1)}, u32[]{:S(2)}, u32[]{:S(2)}) collective-permute-start(bf16[1,2,24,336]{3,2,1,0:T(8,128)(2,1)S(1)} %get-tuple-element.40), channel_id=1, source_target_pairs={{0,2},{1,3},{4,6},{5,7},{8,10},{9,11},{12,14},{13,15},{16,18},{17,... | collective-permute-start | bytes 96776 | tf_op jit(solution)/shard_map/ppermute | solution.py:15
  26.3 23.2 %collective-permute-start.1 = (bf16[1,2,24,336]{3,2,1,0:T(8,128)(2,1)S(1)}, bf16[1,2,24,336]{3,2,1,0:T(8,128)(2,1)S(1)}, u32[]{:S(2)}, u32[]{:S(2)}) collective-permute-start(bf16[1,2,24,336]{3,2,1,0:T(8,128)(2,1)S(1)} %get-tuple-element.41), channel_id=1, source_target_pairs={{2,0},{3,1},{6,4},{7,5},{10,8},{11,9},{14,12},{15,13},{18,16},{19,... | collective-permute-start | bytes 96776 | tf_op jit(solution)/shard_map/ppermute | solution.py:17
  27.7 23.8 %copy-start.10 = (f32[336]{0:T(512)}, f32[336]{0:T(512)S(1)}, u32[]{:S(2)}) copy-start(f32[336]{0:T(512)S(1)} %get-tuple-element.10) | copy-start | bytes 4036
  27.7 23.8 %copy-start.11 = (f32[336]{0:T(512)}, f32[336]{0:T(512)S(1)}, u32[]{:S(2)}) copy-start(f32[336]{0:T(512)S(1)} %get-tuple-element.11) | copy-start | bytes 4036
  27.7 23.8 %copy-start.12 = (f32[336]{0:T(512)}, f32[336]{0:T(512)S(1)}, u32[]{:S(2)}) copy-start(f32[336]{0:T(512)S(1)} %get-tuple-element.12) | copy-start | bytes 4036
  27.7 23.8 %copy-start.13 = (f32[336]{0:T(512)}, f32[336]{0:T(512)S(1)}, u32[]{:S(2)}) copy-start(f32[336]{0:T(512)S(1)} %get-tuple-element.13) | copy-start | bytes 4036
  27.7 23.8 %copy-start.14 = (f32[336]{0:T(512)}, f32[336]{0:T(512)S(1)}, u32[]{:S(2)}) copy-start(f32[336]{0:T(512)S(1)} %get-tuple-element.14) | copy-start | bytes 4036
  27.7 23.8 %copy-start.15 = (f32[336]{0:T(512)}, f32[336]{0:T(512)S(1)}, u32[]{:S(2)}) copy-start(f32[336]{0:T(512)S(1)} %get-tuple-element.15) | copy-start | bytes 4036
  27.8 23.8 %copy-start.16 = (f32[336]{0:T(512)}, f32[336]{0:T(512)S(1)}, u32[]{:S(2)}) copy-start(f32[336]{0:T(512)S(1)} %get-tuple-element.16) | copy-start | bytes 4036
  27.8 23.8 %copy-start.17 = (f32[336]{0:T(512)}, f32[336]{0:T(512)S(1)}, u32[]{:S(2)}) copy-start(f32[336]{0:T(512)S(1)} %get-tuple-element.17) | copy-start | bytes 4036
  27.8 23.8 %copy-start.18 = (f32[336]{0:T(512)}, f32[336]{0:T(512)S(1)}, u32[]{:S(2)}) copy-start(f32[336]{0:T(512)S(1)} %get-tuple-element.18) | copy-start | bytes 4036
  27.8 23.8 %copy-start.19 = (f32[336]{0:T(512)}, f32[336]{0:T(512)S(1)}, u32[]{:S(2)}) copy-start(f32[336]{0:T(512)S(1)} %get-tuple-element.19) | copy-start | bytes 4036
  27.8 23.8 %copy-start.20 = (f32[336]{0:T(512)}, f32[336]{0:T(512)S(1)}, u32[]{:S(2)}) copy-start(f32[336]{0:T(512)S(1)} %get-tuple-element.20) | copy-start | bytes 4036
  27.8 23.8 %copy-start.21 = (f32[336]{0:T(512)}, f32[336]{0:T(512)S(1)}, u32[]{:S(2)}) copy-start(f32[336]{0:T(512)S(1)} %get-tuple-element.21) | copy-start | bytes 4036
  27.9 23.8 %copy-start.22 = (f32[336]{0:T(512)}, f32[336]{0:T(512)S(1)}, u32[]{:S(2)}) copy-start(f32[336]{0:T(512)S(1)} %get-tuple-element.22) | copy-start | bytes 4036
  27.9 23.8 %copy-start.23 = (f32[336]{0:T(512)}, f32[336]{0:T(512)S(1)}, u32[]{:S(2)}) copy-start(f32[336]{0:T(512)S(1)} %get-tuple-element.23) | copy-start | bytes 4036
  27.9 23.8 %copy-start.24 = (f32[336]{0:T(512)}, f32[336]{0:T(512)S(1)}, u32[]{:S(2)}) copy-start(f32[336]{0:T(512)S(1)} %get-tuple-element.24) | copy-start | bytes 4036
  27.9 23.8 %copy-start.25 = (f32[336]{0:T(512)}, f32[336]{0:T(512)S(1)}, u32[]{:S(2)}) copy-start(f32[336]{0:T(512)S(1)} %get-tuple-element.25) | copy-start | bytes 4036
  27.9 23.8 %copy-start.26 = (f32[336]{0:T(512)}, f32[336]{0:T(512)S(1)}, u32[]{:S(2)}) copy-start(f32[336]{0:T(512)S(1)} %get-tuple-element.26) | copy-start | bytes 4036
  27.9 23.8 %copy-start.27 = (f32[336]{0:T(512)}, f32[336]{0:T(512)S(1)}, u32[]{:S(2)}) copy-start(f32[336]{0:T(512)S(1)} %get-tuple-element.27) | copy-start | bytes 4036
  49.5 8.9 %copy-start.2 = (bf16[32,6,24,336]{3,2,1,0:T(8,128)(2,1)S(1)}, bf16[32,6,24,336]{3,2,1,0:T(8,128)(2,1)}, u32[]{:S(2)}) copy-start(bf16[32,6,24,336]{3,2,1,0:T(8,128)(2,1)} %copy-done.1) | copy-start | bytes 9289732
  51.7 1.0 copy-start.4
  58.4 39.7 %copy-start.6 = (f32[672,28]{0,1:T(8,128)S(1)}, f32[672,28]{0,1:T(8,128)}, u32[]{:S(2)}) copy-start(f32[672,28]{0,1:T(8,128)} %param.16) | copy-start | bytes 225796
  85.9 1.8 %copy-start.3 = (bf16[32,6,24,336]{3,2,1,0:T(8,128)(2,1)}, bf16[32,6,24,336]{3,2,1,0:T(8,128)(2,1)S(1)}, u32[]{:S(2)}) copy-start(bf16[32,6,24,336]{3,2,1,0:T(8,128)(2,1)S(1)} %get-tuple-element.33) | copy-start | bytes 9289732
  85.9 63.9 %copy-start.5 = (f32[6,24,336]{2,1,0:T(8,128)S(1)}, f32[6,24,336]{2,1,0:T(8,128)}, u32[]{:S(2)}) copy-start(f32[6,24,336]{2,1,0:T(8,128)} %get-tuple-element.35) | copy-start | bytes 580612
Sparse Core Ops, SparseCore 0:
  116.8 32.9 all-reduce.5
where the time goes:
time: 159 us; the launch traced here: 158 us
  waiting for transfers between devices  48.4 us (30%)
  other arithmetic  43.2 us (27%)
  blocking collectives  24.1 us (15%)
  between operations  15.2 us (10%)
  starting transfers between devices  13.1 us (8%)
  local copies, waits for them, and re-layouts  8.8 us (6%)
  matrix products  5.47 us (3%)
    psum x1, waiting for transfers between devices, on_device(): lax.psum(local_radius.astype(jnp.bfloat16), 'gen').astype(jnp.float32)  28.1 us
    reduce_sum x1, other arithmetic, on_device(): local_radius = jnp.sum(jnp.abs(dw_gens).astype(jnp.float32), axis=0)  27.4 us
    ppermute x2, waiting for transfers between devices, padded_2(): lax.ppermute(tail, axis, [(i, (i + 1) % count) for i in range(ends)])  16.1 us
    psum x1, blocking collectives, on_device(): gate_radius = lax.psum(local_gate, 'gen')  12 us
    ppermute x2, starting transfers between devices, padded_2(): lax.ppermute(tail, axis, [(i, (i + 1) % count) for i in range(ends)])  10.5 us
    psum x1, blocking collectives, on_device(): pool_center, pool_gens = lax.psum((pool_center, pool_gens), 'row')  7.8 us
    unnamed x67, local copies, waits for them, and re-layouts  6.92 us
    concatenate x1, other arithmetic, padded_2(): jnp.concatenate([lax.ppermute(tail, axis, [(i, (i + 1) % count) for i in...  5.74 us
  transfers between devices with their start and end apart: 5, of which 3 were waited for; matrix products, arithmetic and copies ran while one was open for 5% of the time, Pallas kernels for 0%

commit v1 on v0

v1 whole, which is shorter than its diff:
```python
import functools

import jax
import jax.numpy as jnp
from jax import lax
from jax.experimental import pallas as pl
from jax.experimental.pallas import tpu as pltpu
from jax.sharding import PartitionSpec as P

LANES = 128
BLOCK = 4


def conv_rows(src_ref, w_ref, shifted_ref, acc_ref, rows, taps, cols):
    margin = taps // 2
    depth, span, lanes = src_ref.shape
    values = src_ref[...].astype(jnp.float32).reshape(depth * span, lanes)
    col = lax.broadcasted_iota(jnp.int32, (depth * span, lanes), 0) % cols
    for tap_col in range(taps):
        shift = tap_col - margin
        moved = values
        if shift != 0:
            moved = pltpu.roll(values, (-shift) % (depth * span), 0)
            keep = (col + shift >= 0) & (col + shift < cols)
            moved = jnp.where(keep, moved, 0.0)
        shifted_ref[:, :span, :] = moved.astype(jnp.bfloat16).reshape(depth, span, lanes)
        lhs = jnp.concatenate(
            [
                shifted_ref[tap_row : tap_row + rows, :span, :].reshape(rows * span, lanes)
                for tap_row in range(taps)
            ],
            axis=-1,
        )
        part = jnp.dot(lhs, w_ref[tap_col], preferred_element_type=jnp.float32)
        if tap_col == 0:
            acc_ref[: rows * span, :] = part
        else:
            acc_ref[: rows * span, :] += part


def conv_kernel(
    rows, taps, cols, block, chans,
    xg_ref, xc_ref, w_ref, bd_ref,
    dwg_ref, dwc_ref, rad_ref, pg_ref, pc_ref,
    shifted_ref, acc_ref,
):
    step = pl.program_id(0)

    @pl.when(step == 0)
    def _():
        conv_rows(xc_ref, w_ref, shifted_ref, acc_ref, rows, taps, cols)
        total = jnp.zeros((cols, chans), jnp.float32)
        for row in range(rows):
            one = acc_ref[row * 2 * cols : row * 2 * cols + cols, :chans] + bd_ref[...]
            dwc_ref[row] = one
            total = total + one
        pc_ref[...] = jnp.sum(total, axis=0, keepdims=True)
        rad_ref[...] = jnp.zeros_like(rad_ref)

    conv_rows(xg_ref, w_ref, shifted_ref, acc_ref, rows, taps, cols)
    totals = [jnp.zeros((cols, chans), jnp.float32) for _ in range(block)]
    for row in range(rows):
        radius = rad_ref[row]
        for k in range(block):
            start = (row * block + k) * cols
            one = acc_ref[start : start + cols, :chans].astype(jnp.bfloat16)
            dwg_ref[k, row] = one
            wide = one.astype(jnp.float32)
            radius = radius + jnp.abs(wide)
            totals[k] = totals[k] + wide
        rad_ref[row] = radius
    for k in range(block):
        pg_ref[k] = jnp.sum(totals[k], axis=0, keepdims=True)


def conv_call(x_rows, center_rows, weights, b_depth, gens, rows, taps, cols):
    chans = b_depth.shape[0]
    depth = rows + taps - 1
    wide = weights.shape[-1]
    block = BLOCK
    return pl.pallas_call(
        functools.partial(conv_kernel, rows, taps, cols, block, chans),
        grid=(gens // block,),
        in_specs=[
            pl.BlockSpec((depth, block * cols, LANES), lambda i: (0, i, 0)),
            pl.BlockSpec((depth, 2 * cols, LANES), lambda i: (0, 0, 0)),
            pl.BlockSpec(weights.shape, lambda i: (0, 0, 0)),
            pl.BlockSpec((1, chans), lambda i: (0, 0)),
        ],
        out_specs=[
            pl.BlockSpec((block, rows, cols, chans), lambda i: (i, 0, 0, 0)),
            pl.BlockSpec((rows, cols, chans), lambda i: (0, 0, 0)),
            pl.BlockSpec((rows, cols, chans), lambda i: (0, 0, 0)),
            pl.BlockSpec((block, 1, chans), lambda i: (i, 0, 0)),
            pl.BlockSpec((1, chans), lambda i: (0, 0)),
        ],
        out_shape=[
            jax.ShapeDtypeStruct((gens, rows, cols, chans), jnp.bfloat16),
            jax.ShapeDtypeStruct((rows, cols, chans), jnp.float32),
            jax.ShapeDtypeStruct((rows, cols, chans), jnp.float32),
            jax.ShapeDtypeStruct((gens, 1, chans), jnp.float32),
            jax.ShapeDtypeStruct((1, chans), jnp.float32),
        ],
        scratch_shapes=[
            pltpu.VMEM((depth, block * cols, LANES), jnp.bfloat16),
            pltpu.VMEM((rows * block * cols, wide), jnp.float32),
        ],
        compiler_params=pltpu.CompilerParams(
            dimension_semantics=("arbitrary",), vmem_limit_bytes=40 << 20
        ),
        cost_estimate=pl.CostEstimate(
            flops=2 * gens * rows * cols * taps * taps * LANES * wide,
            bytes_accessed=10 << 20,
            transcendentals=0,
        ),
    )(x_rows, center_rows, weights, b_depth[None])


def relax_gate(ex_center, gate_radius):
    low_end = ex_center - gate_radius
    high_end = ex_center + gate_radius
    sig_low = jax.nn.sigmoid(low_end)
    sig_high = jax.nn.sigmoid(high_end)
    slope_val = jnp.minimum(sig_low * (1.0 - sig_low), sig_high * (1.0 - sig_high))
    gate_center = slope_val * ex_center + 0.5 * (
        sig_high + sig_low - slope_val * (high_end + low_end)
    )
    spread_term = 0.5 * (sig_high - sig_low - slope_val * (high_end - low_end))
    return (gate_center, slope_val, spread_term)


def merged_weights(w_expand, b_expand, w_depth):
    taps = w_depth.shape[0]
    c_in, chans = w_expand.shape
    wide = -(-chans // LANES) * LANES
    bias = b_expand.astype(jnp.bfloat16)
    rest = (b_expand - bias.astype(jnp.float32)).astype(jnp.bfloat16)
    mixed = jnp.concatenate([w_expand, bias[None], rest[None]], axis=0)
    mixed = jnp.pad(mixed, ((0, LANES - c_in - 2), (0, wide - chans))).astype(jnp.float32)
    depth = jnp.pad(w_depth, ((0, 0), (0, 0), (0, wide - chans))).transpose(1, 0, 2)
    merged = (depth[:, :, None, :] * mixed[None, None]).astype(jnp.bfloat16)
    return merged.reshape(taps, taps * LANES, wide)


def with_halo(rows_first, axis, margin):
    count = lax.axis_size(axis)
    ends = count - 1
    head = rows_first[:margin]
    tail = rows_first[-margin:]
    above = lax.ppermute(tail, axis, [(i, i + 1) for i in range(ends)])
    below = lax.ppermute(head, axis, [(i + 1, i) for i in range(ends)])
    return above, below


def on_device(
    x_center, x_gens, w_expand, b_expand, w_depth, b_depth, w_reduce, b_reduce, w_excite, b_excite
):
    precise = lax.Precision.HIGHEST
    gens, rows, cols, c_in = x_gens.shape
    chans = w_expand.shape[1]
    taps = w_depth.shape[0]
    margin = taps // 2
    cells = rows * lax.axis_size("row") * cols
    weights = merged_weights(w_expand, b_expand, w_depth)
    flat = x_gens.transpose(1, 0, 2, 3).reshape(rows, gens * cols, c_in)
    ones = jnp.ones((rows, cols, 2), jnp.bfloat16)
    center = jnp.concatenate([x_center, ones], axis=-1)
    above, below = with_halo(flat, "row", margin)
    above_c, below_c = with_halo(center, "row", margin)
    x_rows = jnp.pad(
        jnp.concatenate([above, flat, below], axis=0), ((0, 0), (0, 0), (0, LANES - c_in))
    )
    center_rows = jnp.pad(
        jnp.concatenate([above_c, center, below_c], axis=0),
        ((0, 0), (0, cols), (0, LANES - c_in - 2)),
    )
    dw_gens, dw_center, local_radius, sum_gens, sum_center = conv_call(
        x_rows, center_rows, weights, b_depth, gens, rows, taps, cols
    )
    feat_radius = lax.psum(local_radius.astype(jnp.bfloat16), "gen").astype(jnp.float32)
    pooled = jnp.concatenate([sum_gens[:, 0], sum_center], axis=0) * (1.0 / cells)
    own = lax.dynamic_slice_in_dim(w_reduce, lax.axis_index("ch") * chans, chans, 0)
    squeezed = lax.psum(jnp.dot(pooled, own, precision=precise), ("row", "ch"))
    ex_all = jnp.dot(squeezed, w_excite, precision=precise)
    ex_gens = ex_all[:gens]
    ex_center = ex_all[gens] + jnp.dot(b_reduce, w_excite, precision=precise) + b_excite
    gate_radius = lax.psum(jnp.sum(jnp.abs(ex_gens), axis=0), "gen")
    gate_center, slope_val, spread_term = relax_gate(ex_center, gate_radius)
    gate_gens = slope_val * ex_gens
    gate_total = slope_val * gate_radius + spread_term
    out_center = dw_center * gate_center
    out_gens = (
        dw_center[None] * gate_gens[:, None, None, :] + gate_center * dw_gens.astype(jnp.float32)
    ).astype(jnp.bfloat16)
    out_box = jnp.abs(dw_center) * spread_term + feat_radius * gate_total
    return (out_center, out_gens, out_box)


def solution(mesh):
    in_specs = (
        P(("grp", "row"), None, None),
        P(("grp", "gen"), "row", None, None),
        P(None, "ch"),
        P("ch"),
        P(None, None, "ch"),
        P("ch"),
        P(),
        P(),
        P(None, "ch"),
        P("ch"),
    )
    out_specs = (
        P(("grp", "row"), None, "ch"),
        P(("grp", "gen"), "row", None, "ch"),
        P(("grp", "row"), None, "ch"),
    )
    return jax.shard_map(
        on_device, mesh=mesh, in_specs=in_specs, out_specs=out_specs, check_vma=False
    )
```

time: 159 us -> 123 us (0.77)
  other arithmetic: 43.2 us -> 11.8 us
  Pallas kernels: 0 us -> 25 us
  waiting for transfers between devices: 48.4 us -> 27.9 us
  matrix products: 5.47 us -> 1.31 us
  local copies, waits for them, and re-layouts: 8.8 us -> 6.05 us
    reduce_sum x3 -> x1, other arithmetic: 29.4 us -> 0.02 us  [on_device(): gate_radius = lax.psum(jnp.sum(jnp.abs(ex_gens), axis=0), 'gen')]
    pallas_call x0 -> x1, Pallas kernels: none -> 25 us  [conv_call(): pl.pallas_call(functools.partial(conv_kernel, rows, taps, cols, block, ch...]
    ppermute x4, waiting for transfers between devices: 20.3 us -> 0.01 us  [the longest x2 0.01 us: with_halo(): above = lax.ppermute(tail, axis, [(i, i + 1) for i in range(ends)])]
    unnamed x67 -> x17, local copies, waits for them, and re-layouts: 6.92 us -> 1.83 us
    dot_general x6 -> x3, matrix products: 5.47 us -> 1.31 us  [the longest x1 0.82 us: on_device(): jnp.dot(b_reduce, w_excite, precision=precise)]
    concatenate x1 -> x2, other arithmetic: 5.74 us -> 2.24 us  [the longest x1 2.21 us: on_device(): jnp.concatenate([above, flat, below], axis=0)]
    psum x2, blocking collectives: 19.8 us -> 23 us  [the longest x1 12 us: on_device(): gate_radius = lax.psum(jnp.sum(jnp.abs(ex_gens), axis=0), 'gen')]
    convert_element_type x0 -> x4, other arithmetic: none -> 2.83 us  [the longest x1 0.91 us: merged_weights(): jnp.pad(mixed, ((0, LANES - c_in - 2), (0, wide - chans)))]
  transfers between devices with their start and end apart: 5 -> 5, of which waited for: 3 -> 1; matrix products, arithmetic and copies ran while one was open for 5% -> 9% of each run, Pallas kernels for 0% -> 0%
where the time goes in v1:
time: 123 us
  waiting for transfers between devices  27.9 us (23%)
  Pallas kernels  25 us (20%)
  blocking collectives  23 us (19%)
  between operations  14.3 us (12%)
  starting transfers between devices  13.5 us (11%)
  other arithmetic  11.8 us (10%)
  local copies, waits for them, and re-layouts  6.05 us (5%)
  matrix products  1.31 us (1%)
    psum x1, waiting for transfers between devices, on_device(): lax.psum(local_radius.astype(jnp.bfloat16), 'gen').astype(jnp.float32)  27.9 us
    pallas_call x1, Pallas kernels, conv_call(): pl.pallas_call(functools.partial(conv_kernel, rows, taps, cols, block, ch...  25 us
    psum x1, blocking collectives, on_device(): gate_radius = lax.psum(jnp.sum(jnp.abs(ex_gens), axis=0), 'gen')  12 us
    psum x1, blocking collectives, on_device(): squeezed = lax.psum(jnp.dot(pooled, own, precision=precise), ('row', 'ch'))  11 us
    ppermute x2, starting transfers between devices, with_halo(): above = lax.ppermute(tail, axis, [(i, i + 1) for i in range(ends)])  10.9 us
    convert_element_type x1, other arithmetic, on_device(): out_gens = (dw_center[None] * gate_gens[:, None, None, :] + gate_center *...  4.99 us
    ppermute x2, starting transfers between devices, with_halo(): below = lax.ppermute(head, axis, [(i + 1, i) for i in range(ends)])  2.57 us
  transfers between devices with their start and end apart: 5, of which 1 were waited for; matrix products, arithmetic and copies ran while one was open for 9% of the time, Pallas kernels for 0%

profile of v1, /device:TPU:0, one launch (start us, length us, event | category | flops | bytes accessed | tf_op | source)
XLA Modules:
  0.0 123.0 jit_solution(13255075396213547371)
XLA Ops:
  7.2 0.0 copy-start
  7.2 0.0 copy-start.2
  7.2 0.0 copy-start.4
  7.2 0.0 copy-start.3
  7.2 0.0 copy-start.5
  7.2 0.0 copy-start.6
  7.2 0.0 all-reduce.7.cloned.1.call-start
  7.3 1.3 %fusion.35 = (bf16[2,32,24,112]{3,2,0,1:T(8,128)(2,1)S(1)}, bf16[2,32,24,112]{3,2,0,1:T(8,128)(2,1)S(1)}) fusion(bf16[6,32,24,112]{3,2,0,1:T(8,128)(2,1)} %bitcast.22), kind=kLoop, calls=%fused_computation.62 | loop fusion | bytes 1376256 | tf_op jit(solution)/shard_map/slice | solution.py:149
  8.6 5.6 %collective-permute-start = (bf16[2,768,112]{2,1,0:T(8,128)(2,1)S(1)}, bf16[2,768,112]{2,1,0:T(8,128)(2,1)}, u32[]{:S(2)}, u32[]{:S(2)}) collective-permute-start(bf16[2,768,112]{2,1,0:T(8,128)(2,1)S(1)} %bitcast.24), channel_id=1, source_target_pairs={{0,2},{1,3},{4,6},{5,7},{8,10},{9,11},{12,14},{13,15},{16,18},{17,... | collective-permute-start | bytes 1032200 | tf_op jit(solution)/shard_map/ppermute | solution.py:150
  14.2 0.8 copy.15
  15.0 1.3 %collective-permute-start.1 = (bf16[2,768,112]{2,1,0:T(8,128)(2,1)}, bf16[2,768,112]{2,1,0:T(8,128)(2,1)}, u32[]{:S(2)}, u32[]{:S(2)}) collective-permute-start(bf16[2,768,112]{2,1,0:T(8,128)(2,1)} %bitcast.3), channel_id=1, source_target_pairs={{2,0},{3,1},{6,4},{7,5},{10,8},{11,9},{14,12},{15,13},{18,16},{19,... | collective-permute-start | bytes 1032200 | tf_op jit(solution)/shard_map/ppermute | solution.py:151
  16.3 0.7 pad_slice_fusion.1
  17.0 5.3 %collective-permute-start.2 = (bf16[2,24,114]{2,1,0:T(8,128)(2,1)S(1)}, bf16[2,24,114]{2,1,0:T(8,128)(2,1)S(1)}, u32[]{:S(2)}, u32[]{:S(2)}) collective-permute-start(bf16[2,24,114]{2,1,0:T(8,128)(2,1)S(1)} %get-tuple-element.21), channel_id=1, source_target_pairs={{0,2},{1,3},{4,6},{5,7},{8,10},{9,11},{12,14},{13,15},{16,18},{17,... | collective-permute-start | bytes 32840 | tf_op jit(solution)/shard_map/ppermute | solution.py:150
  22.3 1.3 %collective-permute-start.3 = (bf16[2,24,114]{2,1,0:T(8,128)(2,1)S(1)}, bf16[2,24,114]{2,1,0:T(8,128)(2,1)S(1)}, u32[]{:S(2)}, u32[]{:S(2)}) collective-permute-start(bf16[2,24,114]{2,1,0:T(8,128)(2,1)S(1)} %get-tuple-element.22), channel_id=1, source_target_pairs={{2,0},{3,1},{6,4},{7,5},{10,8},{11,9},{14,12},{15,13},{18,16},{19,... | collective-permute-start | bytes 32840 | tf_op jit(solution)/shard_map/ppermute | solution.py:151
  23.6 0.8 subtract_convert_fusion
  24.4 0.9 fusion.24
  25.3 0.0 copy-done.3
  25.3 0.8 convolution_reduce_fusion
  26.2 0.0 copy-done.5
  26.2 0.0 copy-done.2
  26.2 1.2 copy.14
  27.4 0.0 copy-done.4
  27.5 0.0 copy-done.6
  27.5 0.1 mul.108
  27.6 0.5 fusion.w_ref
  28.1 0.0 collective-permute-done.2
  28.1 0.0 collective-permute-done.3
  28.1 0.0 collective-permute-done
  28.1 0.0 collective-permute-done.1
  28.1 2.2 %fusion.5.xg_ref = bf16[10,768,128]{2,1,0:T(8,128)(2,1)S(1)} fusion(bf16[2,768,112]{2,1,0:T(8,128)(2,1)} %collective-permute-done.1, bf16[6,768,112]{2,1,0:T(8,128)(2,1)} %bitcast.20, bf16[2,768,112]{2,1,0:T(8,128)(2,1)} %collective-permute-done), kind=kLoop, calls=%fused_computation.8 | loop fusion | flops 9830400 | bytes 3686400 | tf_op jit(solution)/shard_map/concatenate | solution.py:171
  30.4 0.0 copy-start.7
  30.4 25.0 %shard_map.121 = (bf16[32,6,24,336]{3,2,1,0:T(8,128)(2,1)S(1)}, f32[6,24,336]{2,1,0:T(8,128)S(1)}, f32[6,24,336]{2,1,0:T(8,128)S(1)}, f32[32,1,336]{2,1,0:T(1,128)S(1)}, f32[1,336]{1,0:T(1,128)S(1)}) custom-call(bf16[10,768,128]{2,1,0:T(8,128)(2,1)S(1)} %fusion.5.xg_ref, bf16[10,48,128]{2,1,0:T(8,128)(2,1)S(1)} %fusion.18.xc_ref, ...), custom_call_target="tpu_custom_call" | custom-call | flops 11324620800 | bytes 10485760 | tf_op jit(solution)/shard_map/pallas_call | solution.py:81
  55.4 0.0 copy-start.1
  55.4 1.8 %copy-done.1 = bf16[32,6,24,336]{3,2,1,0:T(8,128)(2,1)} copy-done((bf16[32,6,24,336]{3,2,1,0:T(8,128)(2,1)}, bf16[32,6,24,336]{3,2,1,0:T(8,128)(2,1)S(1)}, u32[]{:S(2)}) %copy-start.1) | copy-done | bytes 3096600
  57.2 0.0 copy-done
  57.2 0.3 fusion.25
  57.5 11.0 %psum.21 = f32[33,28]{1,0:T(8,128)S(1)} all-reduce(f32[33,28]{1,0:T(8,128)S(1)} %fusion.25), channel_id=1, replica_groups=mesh['grp'=2,'gen'=4,'row'=2,'ch'=2] {'row','ch'}, use_global_device_ids=true, to_apply=%region_0.1 | all-reduce | flops 924 | bytes 7392 | tf_op jit(solution)/shard_map/psum | solution.py:183
  68.5 0.2 fusion.36
  68.8 12.0 %psum.22 = f32[336]{0:T(512)S(1)} all-reduce(f32[336]{0:T(512)S(1)} %abs_reduce_fusion), channel_id=1, replica_groups=mesh['grp'=2,'gen'=4,'row'=2,'ch'=2] {'gen'}, use_global_device_ids=true, to_apply=%region_2.3 | all-reduce | flops 336 | bytes 2688 | tf_op jit(solution)/shard_map/psum | solution.py:187
  80.8 0.0 copy-done.7
  80.8 0.7 convert_element_type.43
  81.5 0.0 all-reduce.7.cloned.1.call-update
  81.5 5.0 %add_convert_fusion = bf16[32,6,24,336]{3,2,1,0:T(8,128)(2,1)} fusion(bf16[32,6,24,336]{3,2,1,0:T(8,128)(2,1)} %copy-done.1, f32[336]{0:T(512)S(1)} %get-tuple-element.24, f32[32,336]{1,0:T(8,128)S(1)} %slice_multiply_fusion, f32[6,24,336]{2,1,0:T(8,128)S(1)} %get-tuple-element.8), kind=kLoop, calls=%fused_computation | loop fusion | flops 7741440 | bytes 6431040 | tf_op jit(solution)/shard_map/convert_element_type | solution.py:194
  86.5 27.9 %all-reduce.7.cloned.1.call-done = bf16[6,24,336]{2,1,0:T(8,128)(2,1)} async-done(((bf16[6,24,336]{2,1,0:T(8,128)(2,1)}), bf16[6,24,336]{2,1,0:T(8,128)(2,1)}) %all-reduce.7.cloned.1.call-update) | async-done | bytes 96784 | tf_op jit(solution)/shard_map/psum | solution.py:180
  114.4 1.7 %multiply_add_fusion = (f32[6,24,336]{2,1,0:T(8,128)}, f32[6,24,336]{2,1,0:T(8,128)}) fusion(bf16[6,24,336]{2,1,0:T(8,128)(2,1)} %all-reduce.7.cloned.1.call-done, f32[6,24,336]{2,1,0:T(8,128)S(1)} %get-tuple-element.8, f32[336]{0:T(512)S(1)} %get-tuple-element.23, f32[336]{0:T(512)S(1)} %get-tuple-element.13, f32[336]{0:T(512)S(1)} %get-tuple-element.24), kind=kLoop, calls=%fused_computation.16 | loop fusion | flops 290304 | bytes 681408 | tf_op jit(solution)/shard_map/add | solution.py:195
  (14 shorter events, 0.2 us)
Async XLA Ops:
  7.2 50.1 %copy-start = (f32[672,28]{0,1:T(8,128)S(1)}, f32[672,28]{0,1:T(8,128)}, u32[]{:S(2)}) copy-start(f32[672,28]{0,1:T(8,128)} %param.16) | copy-start | bytes 225796
  7.2 19.0 %copy-start.2 = (bf16[32,6,24,112]{3,2,1,0:T(8,128)(2,1)S(1)}, bf16[32,6,24,112]{3,2,1,0:T(8,128)(2,1)}, u32[]{:S(2)}) copy-start(bf16[32,6,24,112]{3,2,1,0:T(8,128)(2,1)} %param.11) | copy-start | bytes 3096580
  7.2 20.2 %copy-start.4 = (bf16[6,24,112]{2,1,0:T(8,128)(2,1)S(1)}, bf16[6,24,112]{2,1,0:T(8,128)(2,1)}, u32[]{:S(2)}) copy-start(bf16[6,24,112]{2,1,0:T(8,128)(2,1)} %param.10) | copy-start | bytes 96772
  7.2 18.1 %copy-start.3 = (f32[28,336]{1,0:T(8,128)S(1)}, f32[28,336]{1,0:T(8,128)}, u32[]{:S(2)}) copy-start(f32[28,336]{1,0:T(8,128)} %param.18) | copy-start | bytes 112900
  7.2 19.0 %copy-start.5 = (f32[5,5,336]{2,1,0:T(8,128)S(1)}, f32[5,5,336]{2,1,0:T(8,128)}, u32[]{:S(2)}) copy-start(f32[5,5,336]{2,1,0:T(8,128)} %param.14) | copy-start | bytes 100804
  7.2 20.2 %copy-start.6 = (f32[336]{0:T(512)S(1)}, f32[336]{0:T(512)}, u32[]{:S(2)}) copy-start(f32[336]{0:T(512)} %param.15) | copy-start | bytes 4036
  7.2 107.2 %all-reduce.7.cloned.1.call-start = ((), (), s32[]{:S(2)}) async-start(), calls=%async_computation | async-start | bytes 221184 | tf_op jit(solution)/shard_map/psum | solution.py:180
  8.6 19.5 %collective-permute-start = (bf16[2,768,112]{2,1,0:T(8,128)(2,1)S(1)}, bf16[2,768,112]{2,1,0:T(8,128)(2,1)}, u32[]{:S(2)}, u32[]{:S(2)}) collective-permute-start(bf16[2,768,112]{2,1,0:T(8,128)(2,1)S(1)} %bitcast.24), channel_id=1, source_target_pairs={{0,2},{1,3},{4,6},{5,7},{8,10},{9,11},{12,14},{13,15},{16,18},{17,... | collective-permute-start | bytes 1032200 | tf_op jit(solution)/shard_map/ppermute | solution.py:150
  15.0 13.1 %collective-permute-start.1 = (bf16[2,768,112]{2,1,0:T(8,128)(2,1)}, bf16[2,768,112]{2,1,0:T(8,128)(2,1)}, u32[]{:S(2)}, u32[]{:S(2)}) collective-permute-start(bf16[2,768,112]{2,1,0:T(8,128)(2,1)} %bitcast.3), channel_id=1, source_target_pairs={{2,0},{3,1},{6,4},{7,5},{10,8},{11,9},{14,12},{15,13},{18,16},{19,... | collective-permute-start | bytes 1032200 | tf_op jit(solution)/shard_map/ppermute | solution.py:151
  17.0 11.0 %collective-permute-start.2 = (bf16[2,24,114]{2,1,0:T(8,128)(2,1)S(1)}, bf16[2,24,114]{2,1,0:T(8,128)(2,1)S(1)}, u32[]{:S(2)}, u32[]{:S(2)}) collective-permute-start(bf16[2,24,114]{2,1,0:T(8,128)(2,1)S(1)} %get-tuple-element.21), channel_id=1, source_target_pairs={{0,2},{1,3},{4,6},{5,7},{8,10},{9,11},{12,14},{13,15},{16,18},{17,... | collective-permute-start | bytes 32840 | tf_op jit(solution)/shard_map/ppermute | solution.py:150
  22.3 5.7 %collective-permute-start.3 = (bf16[2,24,114]{2,1,0:T(8,128)(2,1)S(1)}, bf16[2,24,114]{2,1,0:T(8,128)(2,1)S(1)}, u32[]{:S(2)}, u32[]{:S(2)}) collective-permute-start(bf16[2,24,114]{2,1,0:T(8,128)(2,1)S(1)} %get-tuple-element.22), channel_id=1, source_target_pairs={{2,0},{3,1},{6,4},{7,5},{10,8},{11,9},{14,12},{15,13},{18,16},{19,... | collective-permute-start | bytes 32840 | tf_op jit(solution)/shard_map/ppermute | solution.py:151
  30.4 50.4 %copy-start.7 = (f32[336]{0:T(512)S(1)}, f32[336]{0:T(512)}, u32[]{:S(2)}) copy-start(f32[336]{0:T(512)} %param.19) | copy-start | bytes 4036
  55.4 1.8 %copy-start.1 = (bf16[32,6,24,336]{3,2,1,0:T(8,128)(2,1)}, bf16[32,6,24,336]{3,2,1,0:T(8,128)(2,1)S(1)}, u32[]{:S(2)}) copy-start(bf16[32,6,24,336]{3,2,1,0:T(8,128)(2,1)S(1)} %get-tuple-element.11) | copy-start | bytes 9289732
Sparse Core Ops, SparseCore 0:
  81.6 32.7 all-reduce.6

commit v2 on v1

--- a/solution.py
+++ b/solution.py
@@ -7,6 +7,7 @@
 from jax.experimental.pallas import tpu as pltpu
 from jax.sharding import PartitionSpec as P
 
+MESH = pl.DeviceIdType.MESH
 LANES = 128
 BLOCK = 4
 
@@ -129,6 +130,192 @@
     return (gate_center, slope_val, spread_term)
 
 
+def exchange_kernel(
+    gens, rows, cols, count_gen, count_row, count_ch, per,
+    rad_ref, sg_ref, sc_ref, wr_ref, br_ref, we_ref, be_ref,
+    gates_ref, stats_ref, feat_ref,
+    send_rad, recv_rad, full_rad, squeeze, gate,
+    rs_send, rs_recv, ag_send, ag_recv, sq_send, sq_recv, gt_send, gt_recv,
+):
+    my_gen = lax.axis_index("gen")
+    my_row = lax.axis_index("row")
+    my_ch = lax.axis_index("ch")
+    chans = stats_ref.shape[-1]
+    cells = rows * cols * count_row
+    gen_peers = [(off, {"gen": lax.rem(my_gen + off, count_gen)}) for off in range(1, count_gen)]
+    side_peers = []
+    for off_row in range(count_row):
+        for off_ch in range(count_ch):
+            if off_row or off_ch:
+                place = {
+                    "row": lax.rem(my_row + off_row, count_row),
+                    "ch": lax.rem(my_ch + off_ch, count_ch),
+                }
+                side_peers.append((off_row * count_ch + off_ch, place))
+    barrier = pltpu.get_barrier_semaphore()
+    for _, place in gen_peers + side_peers:
+        pl.semaphore_signal(barrier, inc=1, device_id=place, device_id_type=MESH)
+
+    pooled = jnp.concatenate(
+        [sg_ref[...], sc_ref[...], jnp.zeros((7, chans), jnp.float32)], axis=0
+    ) * (1.0 / cells)
+    part = jnp.dot(
+        pooled, wr_ref[...], precision=lax.Precision.HIGHEST, preferred_element_type=jnp.float32
+    )
+    mine = my_row * count_ch + my_ch
+    squeeze[mine] = part
+    tiles = rows * cols // 8
+    send_rad[:tiles] = rad_ref[...].reshape(tiles, 8, chans).astype(jnp.bfloat16)
+    if count_gen * per > tiles:
+        send_rad[tiles:] = jnp.zeros((count_gen * per - tiles, 8, chans), jnp.bfloat16)
+    recv_rad[my_gen] = send_rad[pl.ds(my_gen * per, per)]
+
+    pl.semaphore_wait(barrier, len(gen_peers) + len(side_peers))
+
+    def remote(src, dst, send_sem, recv_sem, place):
+        return pltpu.make_async_remote_copy(
+            src_ref=src, dst_ref=dst, send_sem=send_sem, recv_sem=recv_sem,
+            device_id=place, device_id_type=MESH,
+        )
+
+    sq_copies = [
+        remote(squeeze.at[mine], squeeze.at[mine], sq_send.at[off], sq_recv.at[off], place)
+        for off, place in side_peers
+    ]
+    rs_copies = [
+        remote(
+            send_rad.at[pl.ds(place["gen"] * per, per)], recv_rad.at[my_gen],
+            rs_send.at[off], rs_recv.at[off], place,
+        )
+        for off, place in gen_peers
+    ]
+    for copy in sq_copies + rs_copies:
+        copy.start()
+    for copy in sq_copies:
+        copy.wait()
+    total = squeeze[0]
+    for slot in range(1, count_row * count_ch):
+        total = total + squeeze[slot]
+    row_of = lax.broadcasted_iota(jnp.int32, total.shape, 0)
+    total = total + jnp.where(row_of == gens, br_ref[...], 0.0)
+    ex_all = jnp.dot(
+        total, we_ref[...], precision=lax.Precision.HIGHEST, preferred_element_type=jnp.float32
+    )
+    ex_gens = ex_all[:gens]
+    ex_center = ex_all[gens : gens + 1] + be_ref[...]
+    gate[my_gen] = jnp.sum(jnp.abs(ex_gens), axis=0, keepdims=True)
+    gt_copies = [
+        remote(gate.at[my_gen], gate.at[my_gen], gt_send.at[off], gt_recv.at[off], place)
+        for off, place in gen_peers
+    ]
+    for copy in gt_copies:
+        copy.start()
+
+    for copy in rs_copies:
+        copy.wait()
+    chunk = recv_rad[0].astype(jnp.float32)
+    for slot in range(1, count_gen):
+        chunk = chunk + recv_rad[slot].astype(jnp.float32)
+    own = pl.ds(my_gen * per, per)
+    full_rad[own] = chunk.astype(jnp.bfloat16)
+    ag_copies = [
+        remote(full_rad.at[own], full_rad.at[own], ag_send.at[off], ag_recv.at[off], place)
+        for off, place in gen_peers
+    ]
+    for copy in ag_copies:
+        copy.start()
+
+    for copy in gt_copies:
+        copy.wait()
+    gate_radius = gate[0]
+    for slot in range(1, count_gen):
+        gate_radius = gate_radius + gate[slot]
+    gate_center, slope_val, spread_term = relax_gate(ex_center, gate_radius)
+    gates_ref[...] = slope_val * ex_gens
+    gate_total = slope_val * gate_radius + spread_term
+    stats_ref[0:1] = gate_center
+    stats_ref[1:2] = spread_term
+    stats_ref[2:3] = gate_total
+    for copy in ag_copies:
+        copy.wait()
+    feat_ref[...] = full_rad[:tiles].astype(jnp.float32).reshape(rows, cols, chans)
+
+
+def exchange_call(mesh, radius, sum_gens, sum_center, w_own, b_reduce, w_excite, b_excite):
+    rows, cols, chans = radius.shape
+    gens = sum_gens.shape[0]
+    count_gen, count_row, count_ch = mesh["gen"], mesh["row"], mesh["ch"]
+    per = -(-(rows * cols // 8) // count_gen)
+    units = w_own.shape[1]
+    vmem = pl.BlockSpec(memory_space=pltpu.VMEM)
+    side = count_row * count_ch
+    dma = pltpu.SemaphoreType.DMA
+    return pl.pallas_call(
+        functools.partial(exchange_kernel, gens, rows, cols, count_gen, count_row, count_ch, per),
+        in_specs=[vmem] * 7,
+        out_specs=[vmem] * 3,
+        out_shape=[
+            jax.ShapeDtypeStruct((gens, chans), jnp.float32),
+            jax.ShapeDtypeStruct((3, chans), jnp.float32),
+            jax.ShapeDtypeStruct((rows, cols, chans), jnp.float32),
+        ],
+        scratch_shapes=[
+            pltpu.VMEM((count_gen * per, 8, chans), jnp.bfloat16),
+            pltpu.VMEM((count_gen, per, 8, chans), jnp.bfloat16),
+            pltpu.VMEM((count_gen * per, 8, chans), jnp.bfloat16),
+            pltpu.VMEM((side, gens + 8, units), jnp.float32),
+            pltpu.VMEM((count_gen, 1, chans), jnp.float32),
+            dma((count_gen,)), dma((count_gen,)), dma((count_gen,)), dma((count_gen,)),
+            dma((side,)), dma((side,)), dma((count_gen,)), dma((count_gen,)),
+        ],
+        compiler_params=pltpu.CompilerParams(
+            collective_id=1, has_side_effects=True, vmem_limit_bytes=32 << 20
+        ),
+    )(radius, sum_gens, sum_center, w_own, b_reduce[None], w_excite, b_excite[None])
+
+
+def final_kernel(block, dwg_ref, gates_ref, dwc_ref, feat_ref, stats_ref, oc_ref, og_ref, ob_ref):
+    center = dwc_ref[...]
+    gate_center = stats_ref[0:1]
+
+    @pl.when(pl.program_id(0) == 0)
+    def _():
+        oc_ref[...] = center * gate_center
+        ob_ref[...] = jnp.abs(center) * stats_ref[1:2] + feat_ref[...] * stats_ref[2:3]
+
+    for k in range(block):
+        og_ref[k] = (
+            center * gates_ref[k] + gate_center * dwg_ref[k].astype(jnp.float32)
+        ).astype(jnp.bfloat16)
+
+
+def final_call(dw_gens, gates, dw_center, feat, stats):
+    gens, rows, cols, chans = dw_gens.shape
+    block = 8
+    whole = pl.BlockSpec((rows, cols, chans), lambda i: (0, 0, 0))
+    big = pl.BlockSpec((block, rows, cols, chans), lambda i: (i, 0, 0, 0))
+    return pl.pallas_call(
+        functools.partial(final_kernel, block),
+        grid=(gens // block,),
+        in_specs=[
+            big,
+            pl.BlockSpec((block, 1, chans), lambda i: (i, 0, 0)),
+            whole,
+            whole,
+            pl.BlockSpec((3, chans), lambda i: (0, 0)),
+        ],
+        out_specs=[whole, big, whole],
+        out_shape=[
+            jax.ShapeDtypeStruct((rows, cols, chans), jnp.float32),
+            jax.ShapeDtypeStruct(dw_gens.shape, jnp.bfloat16),
+            jax.ShapeDtypeStruct((rows, cols, chans), jnp.float32),
+        ],
+        compiler_params=pltpu.CompilerParams(
+            dimension_semantics=("arbitrary",), vmem_limit_bytes=32 << 20
+        ),
+    )(dw_gens, gates[:, None], dw_center, feat, stats)
+
+
 def merged_weights(w_expand, b_expand, w_depth):
     taps = w_depth.shape[0]
     c_in, chans = w_expand.shape
@@ -153,14 +340,12 @@
 
 
 def on_device(
-    x_center, x_gens, w_expand, b_expand, w_depth, b_depth, w_reduce, b_reduce, w_excite, b_excite
+    shape, x_center, x_gens, w_expand, b_expand, w_depth, b_depth, w_reduce, b_reduce, w_excite, b_excite
 ):
-    precise = lax.Precision.HIGHEST
     gens, rows, cols, c_in = x_gens.shape
     chans = w_expand.shape[1]
     taps = w_depth.shape[0]
     margin = taps // 2
-    cells = rows * lax.axis_size("row") * cols
     weights = merged_weights(w_expand, b_expand, w_depth)
     flat = x_gens.transpose(1, 0, 2, 3).reshape(rows, gens * cols, c_in)
     ones = jnp.ones((rows, cols, 2), jnp.bfloat16)
@@ -177,23 +362,19 @@
     dw_gens, dw_center, local_radius, sum_gens, sum_center = conv_call(
         x_rows, center_rows, weights, b_depth, gens, rows, taps, cols
     )
-    feat_radius = lax.psum(local_radius.astype(jnp.bfloat16), "gen").astype(jnp.float32)
-    pooled = jnp.concatenate([sum_gens[:, 0], sum_center], axis=0) * (1.0 / cells)
     own = lax.dynamic_slice_in_dim(w_reduce, lax.axis_index("ch") * chans, chans, 0)
-    squeezed = lax.psum(jnp.dot(pooled, own, precision=precise), ("row", "ch"))
-    ex_all = jnp.dot(squeezed, w_excite, precision=precise)
-    ex_gens = ex_all[:gens]
-    ex_center = ex_all[gens] + jnp.dot(b_reduce, w_excite, precision=precise) + b_excite
-    gate_radius = lax.psum(jnp.sum(jnp.abs(ex_gens), axis=0), "gen")
-    gate_center, slope_val, spread_term = relax_gate(ex_center, gate_radius)
-    gate_gens = slope_val * ex_gens
-    gate_total = slope_val * gate_radius + spread_term
-    out_center = dw_center * gate_center
-    out_gens = (
-        dw_center[None] * gate_gens[:, None, None, :] + gate_center * dw_gens.astype(jnp.float32)
-    ).astype(jnp.bfloat16)
-    out_box = jnp.abs(dw_center) * spread_term + feat_radius * gate_total
-    return (out_center, out_gens, out_box)
+    spare = LANES - own.shape[1]
+    gates, stats, feat = exchange_call(
+        shape,
+        local_radius,
+        sum_gens[:, 0],
+        sum_center,
+        jnp.pad(own, ((0, 0), (0, spare))),
+        jnp.pad(b_reduce, (0, spare)),
+        jnp.pad(w_excite, ((0, spare), (0, 0))),
+        b_excite,
+    )
+    return final_call(dw_gens, gates, dw_center, feat, stats)
 
 
 def solution(mesh):
@@ -215,5 +396,5 @@
         P(("grp", "row"), None, "ch"),
     )
     return jax.shard_map(
-        on_device, mesh=mesh, in_specs=in_specs, out_specs=out_specs, check_vma=False
-    )
+        functools.partial(on_device, dict(mesh.shape)), mesh=mesh, in_specs=in_specs, out_specs=out_specs, check_vma=False
+    )

time: 123 us -> 65 us (0.53)
  waiting for transfers between devices: 27.9 us -> 0.44 us
  blocking collectives: 23 us -> 0 us
  Pallas kernels: 25 us -> 40.5 us
  between operations: 14.3 us -> 0.93 us
  other arithmetic: 11.8 us -> 3.13 us
  matrix products: 1.31 us -> 0 us
    psum x1 -> x0, waiting for transfers between devices: 27.9 us -> none  [on_device(): lax.psum(local_radius.astype(jnp.bfloat16), 'gen').astype(jnp.float32)]
    psum x2 -> x0, blocking collectives: 23 us -> none  [the longest x1 12 us: on_device(): gate_radius = lax.psum(jnp.sum(jnp.abs(ex_gens), axis=0), 'gen')]
    pallas_call x0 -> x2, Pallas kernels: none -> 15.7 us  [the longest x1 12.8 us: exchange_call(): pl.pallas_call(functools.partial(exchange_kernel, gens, rows, cols, count...]
    convert_element_type x2 -> x0, other arithmetic: 5.65 us -> none  [the longest x1 4.99 us: on_device(): out_gens = (dw_center[None] * gate_gens[:, None, None, :] + gate_center *...]
    add x2 -> x0, other arithmetic: 1.72 us -> none  [the longest x1 1.7 us: on_device(): out_box = jnp.abs(dw_center) * spread_term + feat_radius * gate_total]
    unnamed x17 -> x16, local copies, waits for them, and re-layouts: 1.83 us -> 0.16 us
    dot_general x3 -> x0, matrix products: 1.31 us -> none  [the longest x1 0.82 us: on_device(): jnp.dot(b_reduce, w_excite, precision=precise)]
  transfers between devices with their start and end apart: 5 -> 4, of which waited for: 1 -> 1; matrix products, arithmetic and copies ran while one was open for 9% -> 8% of each run, Pallas kernels for 0% -> 0%
where the time goes in v2:
time: 65 us; the launch traced here: 64.6 us
  Pallas kernels  40.5 us (62%)
  starting transfers between devices  14 us (22%)
  local copies, waits for them, and re-layouts  5.56 us (9%)
  other arithmetic  3.13 us (5%)
  between operations  0.93 us (1%)
    pallas_call x1, Pallas kernels, conv_call(): pl.pallas_call(functools.partial(conv_kernel, rows, taps, cols, block, ch...  24.8 us
    pallas_call x1, Pallas kernels, exchange_call(): pl.pallas_call(functools.partial(exchange_kernel, gens, rows, cols, count...  12.8 us
    ppermute x2, starting transfers between devices, with_halo(): above = lax.ppermute(tail, axis, [(i, i + 1) for i in range(ends)])  11.5 us
    pallas_call x1, Pallas kernels, final_call(): pl.pallas_call(functools.partial(final_kernel, block), grid=(gens // bloc...  2.9 us
    ppermute x2, starting transfers between devices, with_halo(): below = lax.ppermute(head, axis, [(i + 1, i) for i in range(ends)])  2.57 us
    slice x3, local copies, waits for them, and re-layouts, with_halo(): tail = rows_first[-margin:]  1.95 us
    concatenate x1, other arithmetic, on_device(): jnp.concatenate([above, flat, below], axis=0)  1.85 us
  transfers between devices with their start and end apart: 4, of which 1 were waited for; matrix products, arithmetic and copies ran while one was open for 8% of the time, Pallas kernels for 0%

profile of v2, /device:TPU:0, one launch (start us, length us, event | category | flops | bytes accessed | tf_op | source)
XLA Modules:
  0.0 64.6 jit_solution(13547798951869495413)
XLA Ops:
  0.6 0.0 copy-start
  0.6 0.0 copy-start.1
  0.7 0.0 copy-start.2
  0.7 0.0 copy-start.5
  0.7 0.0 copy-start.4
  0.7 0.0 copy-start.3
  0.7 0.0 copy-start.6
  0.7 1.3 %fusion.25 = (bf16[2,32,24,112]{3,2,0,1:T(8,128)(2,1)S(1)}, bf16[2,32,24,112]{3,2,0,1:T(8,128)(2,1)S(1)}) fusion(bf16[6,32,24,112]{3,2,0,1:T(8,128)(2,1)} %bitcast.19), kind=kLoop, calls=%fused_computation.38 | loop fusion | bytes 1376256 | tf_op jit(solution)/shard_map/slice | solution.py:336
  2.1 5.6 %collective-permute-start = (bf16[2,768,112]{2,1,0:T(8,128)(2,1)S(1)}, bf16[2,768,112]{2,1,0:T(8,128)(2,1)}, u32[]{:S(2)}, u32[]{:S(2)}) collective-permute-start(bf16[2,768,112]{2,1,0:T(8,128)(2,1)S(1)} %bitcast.21), channel_id=1, source_target_pairs={{0,2},{1,3},{4,6},{5,7},{8,10},{9,11},{12,14},{13,15},{16,18},{17,... | collective-permute-start | bytes 1032200 | tf_op jit(solution)/shard_map/ppermute | solution.py:337
  7.7 1.3 %collective-permute-start.1 = (bf16[2,768,112]{2,1,0:T(8,128)(2,1)S(1)}, bf16[2,768,112]{2,1,0:T(8,128)(2,1)}, u32[]{:S(2)}, u32[]{:S(2)}) collective-permute-start(bf16[2,768,112]{2,1,0:T(8,128)(2,1)S(1)} %bitcast.22), channel_id=1, source_target_pairs={{2,0},{3,1},{6,4},{7,5},{10,8},{11,9},{14,12},{15,13},{18,16},{19,... | collective-permute-start | bytes 1032200 | tf_op jit(solution)/shard_map/ppermute | solution.py:338
  9.0 0.0 copy-done.2
  9.0 0.6 pad_slice_fusion.1
  9.6 5.9 %collective-permute-start.2 = (bf16[2,24,114]{2,1,0:T(8,128)(2,1)}, bf16[2,24,114]{2,1,0:T(8,128)(2,1)}, u32[]{:S(2)}, u32[]{:S(2)}) collective-permute-start(bf16[2,24,114]{2,1,0:T(8,128)(2,1)} %get-tuple-element.23), channel_id=1, source_target_pairs={{0,2},{1,3},{4,6},{5,7},{8,10},{9,11},{12,14},{13,15},{16,18},{17,... | collective-permute-start | bytes 32840 | tf_op jit(solution)/shard_map/ppermute | solution.py:337
  15.5 1.3 %collective-permute-start.3 = (bf16[2,24,114]{2,1,0:T(8,128)(2,1)}, bf16[2,24,114]{2,1,0:T(8,128)(2,1)}, u32[]{:S(2)}, u32[]{:S(2)}) collective-permute-start(bf16[2,24,114]{2,1,0:T(8,128)(2,1)} %get-tuple-element.24), channel_id=1, source_target_pairs={{2,0},{3,1},{6,4},{7,5},{10,8},{11,9},{14,12},{15,13},{18,16},{19,... | collective-permute-start | bytes 32840 | tf_op jit(solution)/shard_map/ppermute | solution.py:338
  16.8 0.0 copy-done.5
  16.8 0.0 copy-done.4
  16.9 0.0 copy-done
  16.9 0.1 constant_dynamic-slice_fusion
  17.0 0.0 copy-done.3
  17.0 0.0 copy-done.6
  17.0 0.0 copy-done.1
  17.0 0.2 copy.14
  17.3 0.8 %concatenate.13 = bf16[6,24,114]{2,1,0:T(8,128)(2,1)S(1)} pad(bf16[6,24,112]{2,1,0:T(8,128)(2,1)} %param.10, bf16[]{:T(256)} %constant.4.clone.1), padding=0_0x0_0x0_2 | pad | bytes 65090 | tf_op jit(solution)/shard_map/concatenate | solution.py:352
  18.1 0.7 %broadcast_in_dim.23.bd_ref = f32[1,336]{1,0:T(1,128)S(1)} reshape(f32[336]{0:T(512)} %param.15) | data formatting | bytes 2688 | tf_op jit(solution)/shard_map/broadcast_in_dim | solution.py:117
  18.7 0.1 copy.19
  18.9 0.8 %pad.35.we_ref = f32[128,336]{1,0:T(8,128)S(1)} pad(f32[28,336]{1,0:T(8,128)} %param.18, f32[]{:T(128)} %constant.5.clone.1), padding=0_100x0_0 | pad | bytes 209668 | tf_op jit(solution)/shard_map/jit(_pad)/pad | solution.py:374
  19.7 0.7 %broadcast_in_dim.25.be_ref = f32[1,336]{1,0:T(1,128)S(1)} reshape(f32[336]{0:T(512)} %param.19) | data formatting | bytes 2688 | tf_op jit(solution)/shard_map/broadcast_in_dim | solution.py:274
  20.4 0.1 mul.25
  20.5 0.5 fusion.w_ref
  21.0 0.0 collective-permute-done.2
  21.0 0.4 collective-permute-done.3
  21.4 0.8 %fusion.18.xc_ref = bf16[10,48,128]{2,1,0:T(8,128)(2,1)S(1)} fusion(bf16[2,24,114]{2,1,0:T(8,128)(2,1)} %collective-permute-done.3, bf16[6,24,114]{2,1,0:T(8,128)(2,1)S(1)} %concatenate.13, bf16[2,24,114]{2,1,0:T(8,128)(2,1)} %collective-permute-done.2), kind=kLoop, calls=%fused_computation.24 | loop fusion | flops 921600 | bytes 177600 | tf_op jit(solution)/shard_map/concatenate | solution.py:359
  22.2 0.0 collective-permute-done
  22.2 0.0 collective-permute-done.1
  22.2 1.9 %fusion.5.xg_ref = bf16[10,768,128]{2,1,0:T(8,128)(2,1)S(1)} fusion(bf16[2,768,112]{2,1,0:T(8,128)(2,1)} %collective-permute-done.1, bf16[6,768,112]{2,1,0:T(8,128)(2,1)S(1)} %bitcast.17, bf16[2,768,112]{2,1,0:T(8,128)(2,1)} %collective-permute-done), kind=kLoop, calls=%fused_computation.7 | loop fusion | flops 9830400 | bytes 3686400 | tf_op jit(solution)/shard_map/concatenate | solution.py:356
  24.0 24.8 %shard_map.121 = (bf16[32,6,24,336]{3,2,1,0:T(8,128)(2,1)S(1)}, f32[6,24,336]{2,1,0:T(8,128)S(1)}, f32[6,24,336]{2,1,0:T(8,128)S(1)}, f32[32,1,336]{2,1,0:T(1,128)S(1)}, f32[1,336]{1,0:T(1,128)S(1)}) custom-call(bf16[10,768,128]{2,1,0:T(8,128)(2,1)S(1)} %fusion.5.xg_ref, bf16[10,48,128]{2,1,0:T(8,128)(2,1)S(1)} %fusion.18.xc_ref, ...), custom_call_target="tpu_custom_call" | custom-call | flops 11324620800 | bytes 10485760 | tf_op jit(solution)/shard_map/pallas_call | solution.py:82
  48.9 12.8 %shard_map.122 = (f32[32,336]{1,0:T(8,128)S(1)}, f32[3,336]{1,0:T(4,128)S(1)}, f32[6,24,336]{2,1,0:T(8,128)S(1)}) custom-call(f32[6,24,336]{2,1,0:T(8,128)S(1)} %get-tuple-element.12.rad_ref, f32[32,336]{1,0:T(8,128)S(1)} %bitcast.16, f32[1,336]{1,0:T(1,128)S(1)} %get-tuple-element.14.sc_ref, f32[336,128]{1,0:T(8,128)S(1)} %pad.33.wr_ref, ...), custom_call_target="tpu_custom_call" | custom-call | tf_op jit(solution)/shard_map/pallas_call | solution.py:253
  61.7 2.9 %shard_map.123 = (f32[6,24,336]{2,1,0:T(8,128)}, bf16[32,6,24,336]{3,2,1,0:T(8,128)(2,1)}, f32[6,24,336]{2,1,0:T(8,128)}) custom-call(bf16[32,6,24,336]{3,2,1,0:T(8,128)(2,1)S(1)} %get-tuple-element.11.dwg_ref, f32[32,1,336]{2,1,0:T(1,128)S(1)} %broadcast_in_dim.26.gates_ref, f32[6,24,336]{2,1,0:T(8,128)S(1)} %get-tuple-element.16.dwc_ref, ...), custom_call_target="tpu_custom_call" | custom-call | tf_op jit(solution)/shard_map/pallas_call | solution.py:297
  (12 shorter events, 0.2 us)
Async XLA Ops:
  0.6 16.2 %copy-start = (f32[672,28]{0,1:T(8,128)S(1)}, f32[672,28]{0,1:T(8,128)}, u32[]{:S(2)}) copy-start(f32[672,28]{0,1:T(8,128)} %param.16) | copy-start | bytes 225796
  0.6 16.4 %copy-start.1 = (bf16[32,6,24,112]{3,2,1,0:T(8,128)(2,1)S(1)}, bf16[32,6,24,112]{3,2,1,0:T(8,128)(2,1)}, u32[]{:S(2)}) copy-start(bf16[32,6,24,112]{3,2,1,0:T(8,128)(2,1)} %param.11) | copy-start | bytes 3096580
  0.7 8.4 %copy-start.2 = (bf16[6,24,112]{2,1,0:T(8,128)(2,1)S(1)}, bf16[6,24,112]{2,1,0:T(8,128)(2,1)}, u32[]{:S(2)}) copy-start(bf16[6,24,112]{2,1,0:T(8,128)(2,1)} %param.10) | copy-start | bytes 96772
  0.7 16.1 %copy-start.5 = (f32[336]{0:T(512)S(1)}, f32[336]{0:T(512)}, u32[]{:S(2)}) copy-start(f32[336]{0:T(512)} %param.13) | copy-start | bytes 4036
  0.7 16.2 %copy-start.4 = (f32[5,5,336]{2,1,0:T(8,128)S(1)}, f32[5,5,336]{2,1,0:T(8,128)}, u32[]{:S(2)}) copy-start(f32[5,5,336]{2,1,0:T(8,128)} %param.14) | copy-start | bytes 100804
  0.7 16.3 %copy-start.3 = (bf16[112,336]{1,0:T(8,128)(2,1)S(1)}, bf16[112,336]{1,0:T(8,128)(2,1)}, u32[]{:S(2)}) copy-start(bf16[112,336]{1,0:T(8,128)(2,1)} %param.12) | copy-start | bytes 225796
  0.7 16.3 %copy-start.6 = (f32[28]{0:T(128)S(1)}, f32[28]{0:T(128)}, u32[]{:S(2)}) copy-start(f32[28]{0:T(128)} %param.17) | copy-start | bytes 340
  2.1 20.1 %collective-permute-start = (bf16[2,768,112]{2,1,0:T(8,128)(2,1)S(1)}, bf16[2,768,112]{2,1,0:T(8,128)(2,1)}, u32[]{:S(2)}, u32[]{:S(2)}) collective-permute-start(bf16[2,768,112]{2,1,0:T(8,128)(2,1)S(1)} %bitcast.21), channel_id=1, source_target_pairs={{0,2},{1,3},{4,6},{5,7},{8,10},{9,11},{12,14},{13,15},{16,18},{17,... | collective-permute-start | bytes 1032200 | tf_op jit(solution)/shard_map/ppermute | solution.py:337
  7.7 14.5 %collective-permute-start.1 = (bf16[2,768,112]{2,1,0:T(8,128)(2,1)S(1)}, bf16[2,768,112]{2,1,0:T(8,128)(2,1)}, u32[]{:S(2)}, u32[]{:S(2)}) collective-permute-start(bf16[2,768,112]{2,1,0:T(8,128)(2,1)S(1)} %bitcast.22), channel_id=1, source_target_pairs={{2,0},{3,1},{6,4},{7,5},{10,8},{11,9},{14,12},{15,13},{18,16},{19,... | collective-permute-start | bytes 1032200 | tf_op jit(solution)/shard_map/ppermute | solution.py:338
  9.6 11.3 %collective-permute-start.2 = (bf16[2,24,114]{2,1,0:T(8,128)(2,1)}, bf16[2,24,114]{2,1,0:T(8,128)(2,1)}, u32[]{:S(2)}, u32[]{:S(2)}) collective-permute-start(bf16[2,24,114]{2,1,0:T(8,128)(2,1)} %get-tuple-element.23), channel_id=1, source_target_pairs={{0,2},{1,3},{4,6},{5,7},{8,10},{9,11},{12,14},{13,15},{16,18},{17,... | collective-permute-start | bytes 32840 | tf_op jit(solution)/shard_map/ppermute | solution.py:337
  15.5 5.9 %collective-permute-start.3 = (bf16[2,24,114]{2,1,0:T(8,128)(2,1)}, bf16[2,24,114]{2,1,0:T(8,128)(2,1)}, u32[]{:S(2)}, u32[]{:S(2)}) collective-permute-start(bf16[2,24,114]{2,1,0:T(8,128)(2,1)} %get-tuple-element.24), channel_id=1, source_target_pairs={{2,0},{3,1},{6,4},{7,5},{10,8},{11,9},{14,12},{15,13},{18,16},{19,... | collective-permute-start | bytes 32840 | tf_op jit(solution)/shard_map/ppermute | solution.py:338

commit v3 on v2

--- a/solution.py
+++ b/solution.py
@@ -52,7 +52,7 @@
         conv_rows(xc_ref, w_ref, shifted_ref, acc_ref, rows, taps, cols)
         total = jnp.zeros((cols, chans), jnp.float32)
         for row in range(rows):
-            one = acc_ref[row * 2 * cols : row * 2 * cols + cols, :chans] + bd_ref[...]
+            one = acc_ref[row * 2 * cols : row * 2 * cols + cols, :chans] + bd_ref[0:1]
             dwc_ref[row] = one
             total = total + one
         pc_ref[...] = jnp.sum(total, axis=0, keepdims=True)
@@ -74,8 +74,8 @@
         pg_ref[k] = jnp.sum(totals[k], axis=0, keepdims=True)
 
 
-def conv_call(x_rows, center_rows, weights, b_depth, gens, rows, taps, cols):
-    chans = b_depth.shape[0]
+def conv_call(x_rows, weights, vectors, gens, rows, taps, cols):
+    chans = vectors.shape[1]
     depth = rows + taps - 1
     wide = weights.shape[-1]
     block = BLOCK
@@ -84,9 +84,9 @@
         grid=(gens // block,),
         in_specs=[
             pl.BlockSpec((depth, block * cols, LANES), lambda i: (0, i, 0)),
-            pl.BlockSpec((depth, 2 * cols, LANES), lambda i: (0, 0, 0)),
+            pl.BlockSpec((depth, 2 * cols, LANES), lambda i: (0, gens // 2, 0)),
             pl.BlockSpec(weights.shape, lambda i: (0, 0, 0)),
-            pl.BlockSpec((1, chans), lambda i: (0, 0)),
+            pl.BlockSpec(vectors.shape, lambda i: (0, 0)),
         ],
         out_specs=[
             pl.BlockSpec((block, rows, cols, chans), lambda i: (i, 0, 0, 0)),
@@ -114,7 +114,7 @@
             bytes_accessed=10 << 20,
             transcendentals=0,
         ),
-    )(x_rows, center_rows, weights, b_depth[None])
+    )(x_rows, x_rows, weights, vectors)
 
 
 def relax_gate(ex_center, gate_radius):
@@ -132,7 +132,7 @@
 
 def exchange_kernel(
     gens, rows, cols, count_gen, count_row, count_ch, per,
-    rad_ref, sg_ref, sc_ref, wr_ref, br_ref, we_ref, be_ref,
+    rad_ref, sg_ref, sc_ref, wr_ref, we_ref, vec_ref,
     gates_ref, stats_ref, feat_ref,
     send_rad, recv_rad, full_rad, squeeze, gate,
     rs_send, rs_recv, ag_send, ag_recv, sq_send, sq_recv, gt_send, gt_recv,
@@ -141,6 +141,7 @@
     my_row = lax.axis_index("row")
     my_ch = lax.axis_index("ch")
     chans = stats_ref.shape[-1]
+    units = we_ref.shape[0]
     cells = rows * cols * count_row
     gen_peers = [(off, {"gen": lax.rem(my_gen + off, count_gen)}) for off in range(1, count_gen)]
     side_peers = []
@@ -157,10 +158,12 @@
         pl.semaphore_signal(barrier, inc=1, device_id=place, device_id_type=MESH)
 
     pooled = jnp.concatenate(
-        [sg_ref[...], sc_ref[...], jnp.zeros((7, chans), jnp.float32)], axis=0
+        [sg_ref[...][:, 0], sc_ref[...], jnp.zeros((7, chans), jnp.float32)], axis=0
     ) * (1.0 / cells)
     part = jnp.dot(
-        pooled, wr_ref[...], precision=lax.Precision.HIGHEST, preferred_element_type=jnp.float32
+        pooled, wr_ref[pl.ds(pl.multiple_of(my_ch * chans, 8), chans)],
+        precision=lax.Precision.HIGHEST,
+        preferred_element_type=jnp.float32,
     )
     mine = my_row * count_ch + my_ch
     squeeze[mine] = part
@@ -197,12 +200,12 @@
     for slot in range(1, count_row * count_ch):
         total = total + squeeze[slot]
     row_of = lax.broadcasted_iota(jnp.int32, total.shape, 0)
-    total = total + jnp.where(row_of == gens, br_ref[...], 0.0)
+    total = total + jnp.where(row_of == gens, vec_ref[2:3, :units], 0.0)
     ex_all = jnp.dot(
         total, we_ref[...], precision=lax.Precision.HIGHEST, preferred_element_type=jnp.float32
     )
     ex_gens = ex_all[:gens]
-    ex_center = ex_all[gens : gens + 1] + be_ref[...]
+    ex_center = ex_all[gens : gens + 1] + vec_ref[1:2]
     gate[my_gen] = jnp.sum(jnp.abs(ex_gens), axis=0, keepdims=True)
     gt_copies = [
         remote(gate.at[my_gen], gate.at[my_gen], gt_send.at[off], gt_recv.at[off], place)
@@ -231,7 +234,7 @@
     for slot in range(1, count_gen):
         gate_radius = gate_radius + gate[slot]
     gate_center, slope_val, spread_term = relax_gate(ex_center, gate_radius)
-    gates_ref[...] = slope_val * ex_gens
+    gates_ref[...] = (slope_val * ex_gens)[:, None, :]
     gate_total = slope_val * gate_radius + spread_term
     stats_ref[0:1] = gate_center
     stats_ref[1:2] = spread_term
@@ -241,21 +244,21 @@
     feat_ref[...] = full_rad[:tiles].astype(jnp.float32).reshape(rows, cols, chans)
 
 
-def exchange_call(mesh, radius, sum_gens, sum_center, w_own, b_reduce, w_excite, b_excite):
+def exchange_call(mesh, radius, sum_gens, sum_center, w_reduce, w_excite, vectors):
     rows, cols, chans = radius.shape
     gens = sum_gens.shape[0]
     count_gen, count_row, count_ch = mesh["gen"], mesh["row"], mesh["ch"]
     per = -(-(rows * cols // 8) // count_gen)
-    units = w_own.shape[1]
+    units = w_reduce.shape[1]
     vmem = pl.BlockSpec(memory_space=pltpu.VMEM)
     side = count_row * count_ch
     dma = pltpu.SemaphoreType.DMA
     return pl.pallas_call(
         functools.partial(exchange_kernel, gens, rows, cols, count_gen, count_row, count_ch, per),
-        in_specs=[vmem] * 7,
+        in_specs=[vmem] * 6,
         out_specs=[vmem] * 3,
         out_shape=[
-            jax.ShapeDtypeStruct((gens, chans), jnp.float32),
+            jax.ShapeDtypeStruct((gens, 1, chans), jnp.float32),
             jax.ShapeDtypeStruct((3, chans), jnp.float32),
             jax.ShapeDtypeStruct((rows, cols, chans), jnp.float32),
         ],
@@ -271,7 +274,7 @@
         compiler_params=pltpu.CompilerParams(
             collective_id=1, has_side_effects=True, vmem_limit_bytes=32 << 20
         ),
-    )(radius, sum_gens, sum_center, w_own, b_reduce[None], w_excite, b_excite[None])
+    )(radius, sum_gens, sum_center, w_reduce, w_excite, vectors)
 
 
 def final_kernel(block, dwg_ref, gates_ref, dwc_ref, feat_ref, stats_ref, oc_ref, og_ref, ob_ref):
@@ -313,7 +316,7 @@
         compiler_params=pltpu.CompilerParams(
             dimension_semantics=("arbitrary",), vmem_limit_bytes=32 << 20
         ),
-    )(dw_gens, gates[:, None], dw_center, feat, stats)
+    )(dw_gens, gates, dw_center, feat, stats)
 
 
 def merged_weights(w_expand, b_expand, w_depth):
@@ -329,14 +332,107 @@
     return merged.reshape(taps, taps * LANES, wide)
 
 
-def with_halo(rows_first, axis, margin):
-    count = lax.axis_size(axis)
-    ends = count - 1
-    head = rows_first[:margin]
-    tail = rows_first[-margin:]
-    above = lax.ppermute(tail, axis, [(i, i + 1) for i in range(ends)])
-    below = lax.ppermute(head, axis, [(i + 1, i) for i in range(ends)])
-    return above, below
+def halo_kernel(count_row, count_ch, margin, x_ref, out_ref, zero_ref, local_sem, send_sem, recv_sem, fwd_send, fwd_recv):
+    rows = x_ref.shape[0]
+    per = margin // count_ch
+    my_row = lax.axis_index("row")
+    my_ch = lax.axis_index("ch")
+    has_up = my_row > 0
+    has_down = my_row < count_row - 1
+    barrier = pltpu.get_barrier_semaphore()
+    places = [{"row": lax.rem(my_row + off, count_row)} for off in sorted({1, count_row - 1})]
+    places += [{"ch": lax.rem(my_ch + off, count_ch)} for off in range(1, count_ch)]
+    for place in places:
+        pl.semaphore_signal(barrier, inc=1, device_id=place, device_id_type=MESH)
+
+    inner = pltpu.make_async_copy(x_ref, out_ref.at[pl.ds(margin, rows)], local_sem.at[0])
+    inner.start()
+    zero_ref[...] = jnp.zeros_like(zero_ref)
+    pl.semaphore_wait(barrier, len(places))
+
+    part = my_ch * per
+    above = pl.ds(part, per)
+    below = pl.ds(margin + rows + part, per)
+
+    def sent_down():
+        return pltpu.make_async_remote_copy(
+            src_ref=x_ref.at[pl.ds(rows - margin + part, per)], dst_ref=out_ref.at[above],
+            send_sem=send_sem.at[0], recv_sem=recv_sem.at[0],
+            device_id={"row": lax.rem(my_row + 1, count_row)}, device_id_type=MESH,
+        )
+
+    def sent_up():
+        return pltpu.make_async_remote_copy(
+            src_ref=x_ref.at[pl.ds(part, per)], dst_ref=out_ref.at[below],
+            send_sem=send_sem.at[1], recv_sem=recv_sem.at[1],
+            device_id={"row": lax.rem(my_row + count_row - 1, count_row)}, device_id_type=MESH,
+        )
+
+    def forwards(side):
+        where = (above, below)[side]
+        return [
+            pltpu.make_async_remote_copy(
+                src_ref=out_ref.at[where], dst_ref=out_ref.at[where],
+                send_sem=fwd_send.at[side, off], recv_sem=fwd_recv.at[side, off],
+                device_id={"ch": lax.rem(my_ch + off, count_ch)}, device_id_type=MESH,
+            )
+            for off in range(1, count_ch)
+        ]
+
+    def fill(side):
+        start = (0, margin + rows)[side]
+        return pltpu.make_async_copy(
+            zero_ref, out_ref.at[pl.ds(start, margin)], local_sem.at[1 + side]
+        )
+
+    for present, send in ((has_down, sent_down), (has_up, sent_up)):
+        @pl.when(present)
+        def _(send=send):
+            send().start()
+
+    for side, present, send in ((0, has_up, sent_down), (1, has_down, sent_up)):
+        @pl.when(present)
+        def _(side=side, send=send):
+            send().wait_recv()
+            for copy in forwards(side):
+                copy.start()
+
+        @pl.when(jnp.logical_not(present))
+        def _(side=side):
+            fill(side).start()
+
+    for side, present in ((0, has_up), (1, has_down)):
+        @pl.when(present)
+        def _(side=side):
+            for copy in forwards(side):
+                copy.wait()
+
+        @pl.when(jnp.logical_not(present))
+        def _(side=side):
+            fill(side).wait()
+
+    for present, send in ((has_down, sent_down), (has_up, sent_up)):
+        @pl.when(present)
+        def _(send=send):
+            send().wait_send()
+    inner.wait()
+
+
+def halo_call(mesh, flat, margin):
+    rows, span, lanes = flat.shape
+    anywhere = pl.BlockSpec(memory_space=pl.ANY)
+    dma = pltpu.SemaphoreType.DMA
+    return pl.pallas_call(
+        functools.partial(halo_kernel, mesh["row"], mesh["ch"], margin),
+        in_specs=[anywhere],
+        out_specs=anywhere,
+        out_shape=jax.ShapeDtypeStruct((rows + 2 * margin, span, lanes), flat.dtype),
+        scratch_shapes=[
+            pltpu.VMEM((margin, span, lanes), flat.dtype),
+            dma((3,)), dma((2,)), dma((2,)), dma((2, mesh["ch"])), dma((2, mesh["ch"])),
+        ],
+        compiler_params=pltpu.CompilerParams(collective_id=2, has_side_effects=True),
+    )(flat)
 
 
 def on_device(
@@ -347,32 +443,19 @@
     taps = w_depth.shape[0]
     margin = taps // 2
     weights = merged_weights(w_expand, b_expand, w_depth)
-    flat = x_gens.transpose(1, 0, 2, 3).reshape(rows, gens * cols, c_in)
     ones = jnp.ones((rows, cols, 2), jnp.bfloat16)
     center = jnp.concatenate([x_center, ones], axis=-1)
-    above, below = with_halo(flat, "row", margin)
-    above_c, below_c = with_halo(center, "row", margin)
-    x_rows = jnp.pad(
-        jnp.concatenate([above, flat, below], axis=0), ((0, 0), (0, 0), (0, LANES - c_in))
-    )
-    center_rows = jnp.pad(
-        jnp.concatenate([above_c, center, below_c], axis=0),
-        ((0, 0), (0, cols), (0, LANES - c_in - 2)),
-    )
+    center = jnp.pad(center, ((0, 0), (0, cols), (0, LANES - c_in - 2)))
+    flat = x_gens.transpose(1, 0, 2, 3).reshape(rows, gens * cols, c_in)
+    flat = jnp.concatenate([jnp.pad(flat, ((0, 0), (0, 0), (0, LANES - c_in))), center], axis=1)
+    x_rows = halo_call(shape, flat, margin)
+    units = b_reduce.shape[0]
+    vectors = jnp.stack([b_depth, b_excite, jnp.pad(b_reduce, (0, chans - units))])
     dw_gens, dw_center, local_radius, sum_gens, sum_center = conv_call(
-        x_rows, center_rows, weights, b_depth, gens, rows, taps, cols
-    )
-    own = lax.dynamic_slice_in_dim(w_reduce, lax.axis_index("ch") * chans, chans, 0)
-    spare = LANES - own.shape[1]
+        x_rows, weights, vectors, gens, rows, taps, cols
+    )
     gates, stats, feat = exchange_call(
-        shape,
-        local_radius,
-        sum_gens[:, 0],
-        sum_center,
-        jnp.pad(own, ((0, 0), (0, spare))),
-        jnp.pad(b_reduce, (0, spare)),
-        jnp.pad(w_excite, ((0, spare), (0, 0))),
-        b_excite,
+        shape, local_radius, sum_gens, sum_center, w_reduce, w_excite, vectors
     )
     return final_call(dw_gens, gates, dw_center, feat, stats)
 

time: 65 us -> 100 us (1.54)
  Pallas kernels: 40.5 us -> 81.2 us
  starting transfers between devices: 14 us -> 0 us
  local copies, waits for them, and re-layouts: 5.56 us -> 12.8 us
  other arithmetic: 3.13 us -> 4.93 us
    pallas_call x0 -> x1, Pallas kernels: none -> 39.2 us  [halo_call(): pl.pallas_call(functools.partial(halo_kernel, mesh['row'], mesh['ch'], ma...]
    ppermute x4 -> x0, starting transfers between devices: 14 us -> none  [the longest x2 11.5 us: with_halo(): above = lax.ppermute(tail, axis, [(i, i + 1) for i in range(ends)])]
    unnamed x16 -> x31, local copies, waits for them, and re-layouts: 0.16 us -> 11.5 us
    slice x4 -> x0, local copies, waits for them, and re-layouts: 1.99 us -> none  [the longest x3 1.95 us: with_halo(): tail = rows_first[-margin:]]
    convert_element_type x1, other arithmetic: 0.49 us -> 1.95 us  [merged_weights(): merged = (depth[:, :, None, :] * mixed[None, None]).astype(jnp.bfloat16)]
    broadcast_in_dim x4 -> x0, local copies, waits for them, and re-layouts: 1.41 us -> none  [the longest x1 0.69 us: exchange_call(): b_excite[None]]
    concatenate x2 -> x1, other arithmetic: 2.61 us -> 1.27 us  [on_device(): jnp.concatenate([jnp.pad(flat, ((0, 0), (0, 0), (0, LANES - c_in))), cent...]
  transfers between devices with their start and end apart: 4 -> 0, of which waited for: 1 -> 0; matrix products, arithmetic and copies ran while one was open for 8% -> 0% of each run, Pallas kernels for 0% -> 0%
where the time goes in v3:
time: 100 us; the launch traced here: 99.7 us
  Pallas kernels  81.2 us (81%)
  local copies, waits for them, and re-layouts  12.8 us (13%)
  other arithmetic  4.93 us (5%)
    pallas_call x1, Pallas kernels, halo_call(): pl.pallas_call(functools.partial(halo_kernel, mesh['row'], mesh['ch'], ma...  39.2 us
    pallas_call x1, Pallas kernels, conv_call(): pl.pallas_call(functools.partial(conv_kernel, rows, taps, cols, block, ch...  25.4 us
    pallas_call x1, Pallas kernels, exchange_call(): pl.pallas_call(functools.partial(exchange_kernel, gens, rows, cols, count...  13.7 us
    unnamed x31, local copies, waits for them, and re-layouts  11.5 us
    pallas_call x1, Pallas kernels, final_call(): pl.pallas_call(functools.partial(final_kernel, block), grid=(gens // bloc...  2.9 us

profile of v3, /device:TPU:0, one launch (start us, length us, event | category | flops | bytes accessed | tf_op | source)
XLA Modules:
  0.0 99.7 jit_solution(9650510053152760082)
XLA Ops:
  0.6 0.8 subtract_convert_fusion
  1.4 0.9 fusion.15
  2.3 0.0 copy-start.14
  2.3 0.0 copy-start.12
  2.3 0.0 copy-start.13
  2.4 0.0 copy-start.10
  2.4 0.1 mul.22
  2.4 0.9 pad_bitcast_fusion
  3.4 0.0 copy-start.11
  3.4 1.9 %fusion.w_ref = bf16[5,640,384]{2,1,0:T(8,128)(2,1)} fusion(f32[640,384]{1,0:T(8,128)S(1)} %bitcast.10, f32[5,5,384]{2,1,0:T(8,128)S(1)} %copy.14), kind=kLoop, calls=%fused_computation.1 | loop fusion | flops 2457600 | bytes 3479040 | tf_op jit(solution)/shard_map/convert_element_type | solution.py:331
  5.3 0.0 copy-done.14
  5.4 0.0 copy-done.12
  5.4 0.0 copy-done.13
  5.4 0.0 copy-done.10
  5.4 0.2 copy.13
  5.6 0.0 copy-done.11
  5.7 1.3 %fusion.2.x_ref = bf16[6,816,128]{2,1,0:T(8,128)(2,1)} fusion(bf16[6,768,112]{2,1,0:T(8,128)(2,1)S(1)} %bitcast.9, bf16[6,48,128]{2,1,0:T(8,128)(2,1)S(1)} %fusion.9), kind=kLoop, calls=%fused_computation.4 | loop fusion | flops 3760128 | bytes 2359296 | tf_op jit(solution)/shard_map/concatenate | solution.py:450
  6.9 39.2 %shard_map.121.xg_ref.xc_ref = bf16[10,816,128]{2,1,0:T(8,128)(2,1)} custom-call(bf16[6,816,128]{2,1,0:T(8,128)(2,1)} %fusion.2.x_ref), custom_call_target="tpu_custom_call" | custom-call | tf_op jit(solution)/shard_map/pallas_call | solution.py:425
  46.2 0.0 copy-start
  46.2 1.7 %copy-done = bf16[5,640,384]{2,1,0:T(8,128)(2,1)S(1)} copy-done((bf16[5,640,384]{2,1,0:T(8,128)(2,1)S(1)}, bf16[5,640,384]{2,1,0:T(8,128)(2,1)}, u32[]{:S(2)}) %copy-start) | copy-done | bytes 2457624
  47.8 0.0 copy-start.1
  47.9 1.6 %copy-done.1 = bf16[10,816,128]{2,1,0:T(8,128)(2,1)S(1)} copy-done((bf16[10,816,128]{2,1,0:T(8,128)(2,1)S(1)}, bf16[10,816,128]{2,1,0:T(8,128)(2,1)}, u32[]{:S(2)}) %copy-start.1) | copy-done | bytes 2088984
  49.4 25.4 %shard_map.122 = (bf16[32,6,24,336]{3,2,1,0:T(8,128)(2,1)S(1)}, f32[6,24,336]{2,1,0:T(8,128)S(1)}, f32[6,24,336]{2,1,0:T(8,128)S(1)}, f32[32,1,336]{2,1,0:T(1,128)S(1)}, f32[1,336]{1,0:T(1,128)S(1)}) custom-call(bf16[10,816,128]{2,1,0:T(8,128)(2,1)S(1)} %copy-done.1, bf16[10,816,128]{2,1,0:T(8,128)(2,1)S(1)} %copy-done.1, bf16[5,640,384]{2,1,0:T(8,128)(2,1)S(1)} %copy-done, ...), custom_call_target="tpu_custom_call" | custom-call | flops 11324620800 | bytes 10485760 | tf_op jit(solution)/shard_map/pallas_call | solution.py:82
  74.9 0.0 copy-start.3
  74.9 0.7 copy-done.3
  75.6 0.0 copy-start.5
  75.6 0.7 copy-done.5
  76.2 0.0 copy-start.8
  76.2 0.6 copy-done.8
  76.9 1.8 %copy.15.wr_ref = f32[672,28]{1,0:T(8,128)} copy(f32[672,28]{0,1:T(8,128)} %param.16) | data formatting | bytes 150528 | tf_op args[6]
  78.7 0.0 copy-start.2
  78.7 1.0 copy-done.2
  79.6 0.0 copy-start.4
  79.6 0.9 copy-done.4
  80.6 0.0 copy-start.7
  80.6 0.8 copy-done.7
  81.4 0.0 copy-start.9
  81.4 0.8 copy-done.9
  82.2 13.7 %shard_map.123 = (f32[32,1,336]{2,1,0:T(1,128)S(1)}, f32[3,336]{1,0:T(4,128)S(1)}, f32[6,24,336]{2,1,0:T(8,128)S(1)}) custom-call(f32[6,24,336]{2,1,0:T(8,128)S(1)} %copy-done.4, f32[32,1,336]{2,1,0:T(1,128)S(1)} %copy-done.9, f32[1,336]{1,0:T(1,128)S(1)} %get-tuple-element.14.sc_ref, f32[672,28]{1,0:T(8,128)S(1)} %copy-done.2, f32[28,336]{1,0:T(8,128)S(1)} %copy-done.7, ...), custom_call_target="tpu_custom_call" | custom-call | tf_op jit(solution)/shard_map/pallas_call | solution.py:256
  95.9 0.0 copy-start.6
  95.9 0.9 copy-done.6
  96.8 2.9 %shard_map.124 = (f32[6,24,336]{2,1,0:T(8,128)}, bf16[32,6,24,336]{3,2,1,0:T(8,128)(2,1)}, f32[6,24,336]{2,1,0:T(8,128)}) custom-call(bf16[32,6,24,336]{3,2,1,0:T(8,128)(2,1)S(1)} %get-tuple-element.11.dwg_ref, f32[32,1,336]{2,1,0:T(1,128)S(1)} %get-tuple-element.15.gates_ref, f32[6,24,336]{2,1,0:T(8,128)S(1)} %copy-done.6, ...), custom_call_target="tpu_custom_call" | custom-call | tf_op jit(solution)/shard_map/pallas_call | solution.py:300
  (9 shorter events, 0.1 us)
Async XLA Ops:
  2.3 3.0 %copy-start.14 = (f32[28]{0:T(128)S(1)}, f32[28]{0:T(128)}, u32[]{:S(2)}) copy-start(f32[28]{0:T(128)} %param.17) | copy-start | bytes 340
  2.3 3.0 %copy-start.12 = (f32[336]{0:T(512)S(1)}, f32[336]{0:T(512)}, u32[]{:S(2)}) copy-start(f32[336]{0:T(512)} %param.15) | copy-start | bytes 4036
  2.3 3.0 %copy-start.13 = (f32[336]{0:T(512)S(1)}, f32[336]{0:T(512)}, u32[]{:S(2)}) copy-start(f32[336]{0:T(512)} %param.19) | copy-start | bytes 4036
  2.4 3.1 %copy-start.10 = (bf16[32,6,24,112]{3,2,1,0:T(8,128)(2,1)S(1)}, bf16[32,6,24,112]{3,2,1,0:T(8,128)(2,1)}, u32[]{:S(2)}) copy-start(bf16[32,6,24,112]{3,2,1,0:T(8,128)(2,1)} %param.11) | copy-start | bytes 3096580
  3.4 2.3 %copy-start.11 = (bf16[6,24,112]{2,1,0:T(8,128)(2,1)S(1)}, bf16[6,24,112]{2,1,0:T(8,128)(2,1)}, u32[]{:S(2)}) copy-start(bf16[6,24,112]{2,1,0:T(8,128)(2,1)} %param.10) | copy-start | bytes 96772
  46.2 1.7 %copy-start = (bf16[5,640,384]{2,1,0:T(8,128)(2,1)S(1)}, bf16[5,640,384]{2,1,0:T(8,128)(2,1)}, u32[]{:S(2)}) copy-start(bf16[5,640,384]{2,1,0:T(8,128)(2,1)} %fusion.w_ref) | copy-start | bytes 7372804
  47.8 1.6 %copy-start.1 = (bf16[10,816,128]{2,1,0:T(8,128)(2,1)S(1)}, bf16[10,816,128]{2,1,0:T(8,128)(2,1)}, u32[]{:S(2)}) copy-start(bf16[10,816,128]{2,1,0:T(8,128)(2,1)} %shard_map.121.xg_ref.xc_ref) | copy-start | bytes 6266884
  74.9 0.7 copy-start.3
  75.6 0.7 copy-start.5
  76.2 0.6 copy-start.8
  78.7 1.0 copy-start.2
  79.6 0.9 copy-start.4
  80.6 0.8 copy-start.7
  81.4 0.8 copy-start.9
  95.9 0.9 copy-start.6

commit v4 on v3

--- a/solution.py
+++ b/solution.py
@@ -12,10 +12,10 @@
 BLOCK = 4
 
 
-def conv_rows(src_ref, w_ref, shifted_ref, acc_ref, rows, taps, cols):
+def conv_rows(source, w_ref, shifted_ref, acc_ref, rows, taps, cols):
     margin = taps // 2
-    depth, span, lanes = src_ref.shape
-    values = src_ref[...].astype(jnp.float32).reshape(depth * span, lanes)
+    depth, span, lanes = source.shape
+    values = source.astype(jnp.float32).reshape(depth * span, lanes)
     col = lax.broadcasted_iota(jnp.int32, (depth * span, lanes), 0) % cols
     for tap_col in range(taps):
         shift = tap_col - margin
@@ -41,7 +41,7 @@
 
 def conv_kernel(
     rows, taps, cols, block, chans,
-    xg_ref, xc_ref, w_ref, bd_ref,
+    x_ref, w_ref, bd_ref,
     dwg_ref, dwc_ref, rad_ref, pg_ref, pc_ref,
     shifted_ref, acc_ref,
 ):
@@ -49,7 +49,7 @@
 
     @pl.when(step == 0)
     def _():
-        conv_rows(xc_ref, w_ref, shifted_ref, acc_ref, rows, taps, cols)
+        conv_rows(x_ref[:, -2 * cols :], w_ref, shifted_ref, acc_ref, rows, taps, cols)
         total = jnp.zeros((cols, chans), jnp.float32)
         for row in range(rows):
             one = acc_ref[row * 2 * cols : row * 2 * cols + cols, :chans] + bd_ref[0:1]
@@ -58,7 +58,9 @@
         pc_ref[...] = jnp.sum(total, axis=0, keepdims=True)
         rad_ref[...] = jnp.zeros_like(rad_ref)
 
-    conv_rows(xg_ref, w_ref, shifted_ref, acc_ref, rows, taps, cols)
+    span = block * cols
+    here = pl.ds(pl.multiple_of(step * span, span), span)
+    conv_rows(x_ref[:, here], w_ref, shifted_ref, acc_ref, rows, taps, cols)
     totals = [jnp.zeros((cols, chans), jnp.float32) for _ in range(block)]
     for row in range(rows):
         radius = rad_ref[row]
@@ -83,9 +85,8 @@
         functools.partial(conv_kernel, rows, taps, cols, block, chans),
         grid=(gens // block,),
         in_specs=[
-            pl.BlockSpec((depth, block * cols, LANES), lambda i: (0, i, 0)),
-            pl.BlockSpec((depth, 2 * cols, LANES), lambda i: (0, gens // 2, 0)),
-            pl.BlockSpec(weights.shape, lambda i: (0, 0, 0)),
+            pl.BlockSpec(memory_space=pltpu.VMEM),
+            pl.BlockSpec(memory_space=pltpu.VMEM),
             pl.BlockSpec(vectors.shape, lambda i: (0, 0)),
         ],
         out_specs=[
@@ -107,14 +108,14 @@
             pltpu.VMEM((rows * block * cols, wide), jnp.float32),
         ],
         compiler_params=pltpu.CompilerParams(
-            dimension_semantics=("arbitrary",), vmem_limit_bytes=40 << 20
+            dimension_semantics=("arbitrary",), vmem_limit_bytes=20 << 20
         ),
         cost_estimate=pl.CostEstimate(
             flops=2 * gens * rows * cols * taps * taps * LANES * wide,
             bytes_accessed=10 << 20,
             transcendentals=0,
         ),
-    )(x_rows, x_rows, weights, vectors)
+    )(x_rows, weights, vectors)
 
 
 def relax_gate(ex_center, gate_radius):
@@ -160,8 +161,13 @@
     pooled = jnp.concatenate(
         [sg_ref[...][:, 0], sc_ref[...], jnp.zeros((7, chans), jnp.float32)], axis=0
     ) * (1.0 / cells)
-    part = jnp.dot(
-        pooled, wr_ref[pl.ds(pl.multiple_of(my_ch * chans, 8), chans)],
+    own = wr_ref[:, :chans]
+    for other in range(1, count_ch):
+        own = jnp.where(my_ch == other, wr_ref[:, other * chans : (other + 1) * chans], own)
+    part = lax.dot_general(
+        pooled,
+        own,
+        (((1,), (1,)), ((), ())),
         precision=lax.Precision.HIGHEST,
         preferred_element_type=jnp.float32,
     )
@@ -249,7 +255,7 @@
     gens = sum_gens.shape[0]
     count_gen, count_row, count_ch = mesh["gen"], mesh["row"], mesh["ch"]
     per = -(-(rows * cols // 8) // count_gen)
-    units = w_reduce.shape[1]
+    units = w_excite.shape[0]
     vmem = pl.BlockSpec(memory_space=pltpu.VMEM)
     side = count_row * count_ch
     dma = pltpu.SemaphoreType.DMA
@@ -272,7 +278,7 @@
             dma((side,)), dma((side,)), dma((count_gen,)), dma((count_gen,)),
         ],
         compiler_params=pltpu.CompilerParams(
-            collective_id=1, has_side_effects=True, vmem_limit_bytes=32 << 20
+            collective_id=1, has_side_effects=True, vmem_limit_bytes=12 << 20
         ),
     )(radius, sum_gens, sum_center, w_reduce, w_excite, vectors)
 
@@ -314,7 +320,7 @@
             jax.ShapeDtypeStruct((rows, cols, chans), jnp.float32),
         ],
         compiler_params=pltpu.CompilerParams(
-            dimension_semantics=("arbitrary",), vmem_limit_bytes=32 << 20
+            dimension_semantics=("arbitrary",), vmem_limit_bytes=12 << 20
         ),
     )(dw_gens, gates, dw_center, feat, stats)
 
@@ -332,7 +338,7 @@
     return merged.reshape(taps, taps * LANES, wide)
 
 
-def halo_kernel(count_row, count_ch, margin, x_ref, out_ref, zero_ref, local_sem, send_sem, recv_sem, fwd_send, fwd_recv):
+def halo_kernel(count_row, count_ch, margin, x_ref, out_ref, send_sem, recv_sem, fwd_send, fwd_recv):
     rows = x_ref.shape[0]
     per = margin // count_ch
     my_row = lax.axis_index("row")
@@ -345,9 +351,6 @@
     for place in places:
         pl.semaphore_signal(barrier, inc=1, device_id=place, device_id_type=MESH)
 
-    inner = pltpu.make_async_copy(x_ref, out_ref.at[pl.ds(margin, rows)], local_sem.at[0])
-    inner.start()
-    zero_ref[...] = jnp.zeros_like(zero_ref)
     pl.semaphore_wait(barrier, len(places))
 
     part = my_ch * per
@@ -379,16 +382,12 @@
             for off in range(1, count_ch)
         ]
 
-    def fill(side):
-        start = (0, margin + rows)[side]
-        return pltpu.make_async_copy(
-            zero_ref, out_ref.at[pl.ds(start, margin)], local_sem.at[1 + side]
-        )
-
     for present, send in ((has_down, sent_down), (has_up, sent_up)):
         @pl.when(present)
         def _(send=send):
             send().start()
+
+    out_ref[margin : margin + rows] = x_ref[...]
 
     for side, present, send in ((0, has_up, sent_down), (1, has_down, sent_up)):
         @pl.when(present)
@@ -399,7 +398,8 @@
 
         @pl.when(jnp.logical_not(present))
         def _(side=side):
-            fill(side).start()
+            start = (0, margin + rows)[side]
+            out_ref[start : start + margin] = jnp.zeros((margin,) + x_ref.shape[1:], x_ref.dtype)
 
     for side, present in ((0, has_up), (1, has_down)):
         @pl.when(present)
@@ -407,20 +407,15 @@
             for copy in forwards(side):
                 copy.wait()
 
-        @pl.when(jnp.logical_not(present))
-        def _(side=side):
-            fill(side).wait()
-
     for present, send in ((has_down, sent_down), (has_up, sent_up)):
         @pl.when(present)
         def _(send=send):
             send().wait_send()
-    inner.wait()
 
 
 def halo_call(mesh, flat, margin):
     rows, span, lanes = flat.shape
-    anywhere = pl.BlockSpec(memory_space=pl.ANY)
+    anywhere = pl.BlockSpec(memory_space=pltpu.VMEM)
     dma = pltpu.SemaphoreType.DMA
     return pl.pallas_call(
         functools.partial(halo_kernel, mesh["row"], mesh["ch"], margin),
@@ -428,10 +423,11 @@
         out_specs=anywhere,
         out_shape=jax.ShapeDtypeStruct((rows + 2 * margin, span, lanes), flat.dtype),
         scratch_shapes=[
-            pltpu.VMEM((margin, span, lanes), flat.dtype),
-            dma((3,)), dma((2,)), dma((2,)), dma((2, mesh["ch"])), dma((2, mesh["ch"])),
-        ],
-        compiler_params=pltpu.CompilerParams(collective_id=2, has_side_effects=True),
+            dma((2,)), dma((2,)), dma((2, mesh["ch"])), dma((2, mesh["ch"])),
+        ],
+        compiler_params=pltpu.CompilerParams(
+            collective_id=2, has_side_effects=True, vmem_limit_bytes=12 << 20
+        ),
     )(flat)
 
 
@@ -455,7 +451,7 @@
         x_rows, weights, vectors, gens, rows, taps, cols
     )
     gates, stats, feat = exchange_call(
-        shape, local_radius, sum_gens, sum_center, w_reduce, w_excite, vectors
+        shape, local_radius, sum_gens, sum_center, w_reduce.T, w_excite, vectors
     )
     return final_call(dw_gens, gates, dw_center, feat, stats)
 

time: 100 us -> 57.9 us (0.58)
  Pallas kernels: 81.2 us -> 50.3 us
  local copies, waits for them, and re-layouts: 12.8 us -> 3.27 us
  other arithmetic: 4.93 us -> 3.22 us
    pallas_call x1, Pallas kernels: 39.2 us -> 10 us  [halo_call(): pl.pallas_call(functools.partial(halo_kernel, mesh['row'], mesh['ch'], ma...]
    unnamed x31 -> x6, local copies, waits for them, and re-layouts: 11.5 us -> 0.02 us
    another operation x3, local copies, waits for them, and re-layouts: 0.01 us -> 1.47 us  [on_device(): jnp.stack([b_depth, b_excite, jnp.pad(b_reduce, (0, chans - units))])]
    convert_element_type x1, other arithmetic: 1.95 us -> 0.51 us  [merged_weights(): merged = (depth[:, :, None, :] * mixed[None, None]).astype(jnp.bfloat16)]
    pallas_call x1, Pallas kernels: 13.7 us -> 12.6 us  [exchange_call(): pl.pallas_call(functools.partial(exchange_kernel, gens, rows, cols, count...]
    concatenate x1, other arithmetic: 1.27 us -> 0.23 us  [on_device(): jnp.concatenate([jnp.pad(flat, ((0, 0), (0, 0), (0, LANES - c_in))), cent...]
where the time goes in v4:
time: 57.9 us; the launch traced here: 57.6 us
  Pallas kernels  50.3 us (87%)
  local copies, waits for them, and re-layouts  3.27 us (6%)
  other arithmetic  3.22 us (6%)
  between operations  0.74 us (1%)
    pallas_call x1, Pallas kernels, conv_call(): pl.pallas_call(functools.partial(conv_kernel, rows, taps, cols, block, ch...  24.8 us
    pallas_call x1, Pallas kernels, exchange_call(): pl.pallas_call(functools.partial(exchange_kernel, gens, rows, cols, count...  12.6 us
    pallas_call x1, Pallas kernels, halo_call(): pl.pallas_call(functools.partial(halo_kernel, mesh['row'], mesh['ch'], ma...  10 us
    pallas_call x1, Pallas kernels, final_call(): pl.pallas_call(functools.partial(final_kernel, block), grid=(gens // bloc...  2.91 us
    another operation x3, local copies, waits for them, and re-layouts, on_device(): jnp.stack([b_depth, b_excite, jnp.pad(b_reduce, (0, chans - units))])  1.47 us

profile of v4, /device:TPU:0, one launch (start us, length us, event | category | flops | bytes accessed | tf_op | source)
XLA Modules:
  0.0 57.6 jit_solution(15359004873694455816)
XLA Ops:
  0.6 0.0 copy-start.2
  0.6 0.8 %stack.12 = f32[1,336]{1,0:T(1,128)S(1)} reshape(f32[336]{0:T(512)} %param.15) | data formatting | bytes 2688 | tf_op jit(solution)/shard_map/stack | solution.py:449
  1.4 0.7 %stack.13 = f32[1,336]{1,0:T(1,128)S(1)} reshape(f32[336]{0:T(512)} %param.19) | data formatting | bytes 2688 | tf_op jit(solution)/shard_map/stack | solution.py:449
  2.1 0.7 %pad.25 = f32[336]{0:T(512)S(1)} pad(f32[28]{0:T(128)} %param.17, f32[]{:T(128)} %constant.6.clone.1), padding=0_308 | pad | bytes 1460 | tf_op jit(solution)/shard_map/jit(_pad)/pad | solution.py:449
  2.8 0.8 %subtract_convert_fusion = (bf16[336]{0:T(512)(128)(2,1)S(1)}, bf16[336]{0:T(512)(128)(2,1)S(1)}) fusion(f32[336]{0:T(512)} %param.13), kind=kLoop, calls=%fused_computation.24 | loop fusion | flops 1344 | bytes 2688 | tf_op jit(solution)/shard_map/convert_element_type | solution.py:333
  3.6 0.8 %pad_bitcast_fusion = f32[5,5,384]{2,0,1:T(8,128)S(1)} fusion(f32[5,5,336]{2,1,0:T(8,128)} %param.14), kind=kLoop, calls=%fused_computation.22 | loop fusion | bytes 72000 | tf_op jit(solution)/shard_map/transpose | solution.py:336
  4.4 0.8 %fusion.9 = bf16[6,48,128]{2,1,0:T(8,128)(2,1)S(1)} fusion(bf16[6,24,112]{2,1,0:T(8,128)(2,1)} %param.10), kind=kLoop, calls=%fused_computation.15 | loop fusion | flops 184320 | bytes 105984 | tf_op jit(solution)/shard_map/jit(_pad)/pad | solution.py:444
  5.2 0.9 %fusion.15 = f32[128,384]{1,0:T(8,128)S(1)} fusion(bf16[1,336]{1,0:T(2,128)(2,1)S(1)} %broadcast_in_dim.10, bf16[1,336]{1,0:T(2,128)(2,1)S(1)} %broadcast_in_dim.4, bf16[112,336]{1,0:T(8,128)(2,1)} %param.12), kind=kLoop, calls=%fused_computation.21 | loop fusion | flops 737280 | bytes 273216 | tf_op jit(solution)/shard_map/convert_element_type | solution.py:335
  6.1 0.1 mul.22
  6.2 0.0 copy-done.2
  6.2 0.2 copy.13
  6.4 0.2 fusion.2.x_ref
  6.6 10.0 %shard_map.121.x_ref = bf16[10,816,128]{2,1,0:T(8,128)(2,1)S(1)} custom-call(bf16[6,816,128]{2,1,0:T(8,128)(2,1)S(1)} %fusion.2.x_ref), custom_call_target="tpu_custom_call" | custom-call | tf_op jit(solution)/shard_map/pallas_call | solution.py:420
  16.7 0.5 fusion.w_ref
  17.2 0.0 copy-start
  17.2 0.0 copy-start.1
  17.2 24.8 %shard_map.122 = (bf16[32,6,24,336]{3,2,1,0:T(8,128)(2,1)S(1)}, f32[6,24,336]{2,1,0:T(8,128)S(1)}, f32[6,24,336]{2,1,0:T(8,128)S(1)}, f32[32,1,336]{2,1,0:T(1,128)S(1)}, f32[1,336]{1,0:T(1,128)S(1)}) custom-call(bf16[10,816,128]{2,1,0:T(8,128)(2,1)S(1)} %shard_map.121.x_ref, bf16[5,640,384]{2,1,0:T(8,128)(2,1)S(1)} %fusion.w_ref, ...), custom_call_target="tpu_custom_call" | custom-call | flops 11324620800 | bytes 10485760 | tf_op jit(solution)/shard_map/pallas_call | solution.py:84
  42.0 0.0 copy-done
  42.0 0.0 copy-done.1
  42.1 12.6 %shard_map.123 = (f32[32,1,336]{2,1,0:T(1,128)S(1)}, f32[3,336]{1,0:T(4,128)S(1)}, f32[6,24,336]{2,1,0:T(8,128)S(1)}) custom-call(f32[6,24,336]{2,1,0:T(8,128)S(1)} %get-tuple-element.12.rad_ref, f32[32,1,336]{2,1,0:T(1,128)S(1)} %get-tuple-element.13.sg_ref, f32[1,336]{1,0:T(1,128)S(1)} %get-tuple-element.14.sc_ref, f32[28,672]{1,0:T(8,128)S(1)} %bitcast.10, ...), custom_call_target="tpu_custom_call" | custom-call | tf_op jit(solution)/shard_map/pallas_call | solution.py:262
  54.6 2.9 %shard_map.124 = (f32[6,24,336]{2,1,0:T(8,128)}, bf16[32,6,24,336]{3,2,1,0:T(8,128)(2,1)}, f32[6,24,336]{2,1,0:T(8,128)}) custom-call(bf16[32,6,24,336]{3,2,1,0:T(8,128)(2,1)S(1)} %get-tuple-element.11.dwg_ref, f32[32,1,336]{2,1,0:T(1,128)S(1)} %get-tuple-element.15.gates_ref, f32[6,24,336]{2,1,0:T(8,128)S(1)} %get-tuple-element.16.dwc_ref, ...), custom_call_target="tpu_custom_call" | custom-call | tf_op jit(solution)/shard_map/pallas_call | solution.py:306
  (5 shorter events, 0.0 us)
Async XLA Ops:
  0.6 5.6 %copy-start.2 = (bf16[32,6,24,112]{3,2,1,0:T(8,128)(2,1)S(1)}, bf16[32,6,24,112]{3,2,1,0:T(8,128)(2,1)}, u32[]{:S(2)}) copy-start(bf16[32,6,24,112]{3,2,1,0:T(8,128)(2,1)} %param.11) | copy-start | bytes 3096580
  17.2 24.8 %copy-start = (f32[672,28]{0,1:T(8,128)S(1)}, f32[672,28]{0,1:T(8,128)}, u32[]{:S(2)}) copy-start(f32[672,28]{0,1:T(8,128)} %param.16) | copy-start | bytes 225796
  17.2 24.8 %copy-start.1 = (f32[28,336]{1,0:T(8,128)S(1)}, f32[28,336]{1,0:T(8,128)}, u32[]{:S(2)}) copy-start(f32[28,336]{1,0:T(8,128)} %we_ref.1) | copy-start | bytes 112900

commit v5 on v4

--- a/solution.py
+++ b/solution.py
@@ -9,7 +9,7 @@
 
 MESH = pl.DeviceIdType.MESH
 LANES = 128
-BLOCK = 4
+BLOCK = 8
 
 
 def conv_rows(source, w_ref, shifted_ref, acc_ref, rows, taps, cols):
@@ -24,19 +24,16 @@
             moved = pltpu.roll(values, (-shift) % (depth * span), 0)
             keep = (col + shift >= 0) & (col + shift < cols)
             moved = jnp.where(keep, moved, 0.0)
-        shifted_ref[:, :span, :] = moved.astype(jnp.bfloat16).reshape(depth, span, lanes)
-        lhs = jnp.concatenate(
-            [
-                shifted_ref[tap_row : tap_row + rows, :span, :].reshape(rows * span, lanes)
-                for tap_row in range(taps)
-            ],
-            axis=-1,
-        )
-        part = jnp.dot(lhs, w_ref[tap_col], preferred_element_type=jnp.float32)
-        if tap_col == 0:
-            acc_ref[: rows * span, :] = part
-        else:
-            acc_ref[: rows * span, :] += part
+        shifted_ref[tap_col, :, :span, :] = moved.astype(jnp.bfloat16).reshape(depth, span, lanes)
+    lhs = jnp.concatenate(
+        [
+            shifted_ref[tap_col, tap_row : tap_row + rows, :span, :].reshape(rows * span, lanes)
+            for tap_col in range(taps)
+            for tap_row in range(taps)
+        ],
+        axis=-1,
+    )
+    acc_ref[: rows * span, :] = jnp.dot(lhs, w_ref[...], preferred_element_type=jnp.float32)
 
 
 def conv_kernel(
@@ -52,7 +49,7 @@
         conv_rows(x_ref[:, -2 * cols :], w_ref, shifted_ref, acc_ref, rows, taps, cols)
         total = jnp.zeros((cols, chans), jnp.float32)
         for row in range(rows):
-            one = acc_ref[row * 2 * cols : row * 2 * cols + cols, :chans] + bd_ref[0:1]
+            one = acc_ref[row * 2 * cols : row * 2 * cols + cols, :chans] + bd_ref[...][None, :]
             dwc_ref[row] = one
             total = total + one
         pc_ref[...] = jnp.sum(total, axis=0, keepdims=True)
@@ -76,8 +73,8 @@
         pg_ref[k] = jnp.sum(totals[k], axis=0, keepdims=True)
 
 
-def conv_call(x_rows, weights, vectors, gens, rows, taps, cols):
-    chans = vectors.shape[1]
+def conv_call(x_rows, weights, b_depth, gens, rows, taps, cols):
+    chans = b_depth.shape[0]
     depth = rows + taps - 1
     wide = weights.shape[-1]
     block = BLOCK
@@ -87,7 +84,7 @@
         in_specs=[
             pl.BlockSpec(memory_space=pltpu.VMEM),
             pl.BlockSpec(memory_space=pltpu.VMEM),
-            pl.BlockSpec(vectors.shape, lambda i: (0, 0)),
+            pl.BlockSpec(memory_space=pltpu.VMEM),
         ],
         out_specs=[
             pl.BlockSpec((block, rows, cols, chans), lambda i: (i, 0, 0, 0)),
@@ -104,18 +101,18 @@
             jax.ShapeDtypeStruct((1, chans), jnp.float32),
         ],
         scratch_shapes=[
-            pltpu.VMEM((depth, block * cols, LANES), jnp.bfloat16),
+            pltpu.VMEM((taps, depth, block * cols, LANES), jnp.bfloat16),
             pltpu.VMEM((rows * block * cols, wide), jnp.float32),
         ],
         compiler_params=pltpu.CompilerParams(
-            dimension_semantics=("arbitrary",), vmem_limit_bytes=20 << 20
+            dimension_semantics=("arbitrary",), vmem_limit_bytes=32 << 20
         ),
         cost_estimate=pl.CostEstimate(
             flops=2 * gens * rows * cols * taps * taps * LANES * wide,
             bytes_accessed=10 << 20,
             transcendentals=0,
         ),
-    )(x_rows, weights, vectors)
+    )(x_rows, weights, b_depth)
 
 
 def relax_gate(ex_center, gate_radius):
@@ -133,7 +130,7 @@
 
 def exchange_kernel(
     gens, rows, cols, count_gen, count_row, count_ch, per,
-    rad_ref, sg_ref, sc_ref, wr_ref, we_ref, vec_ref,
+    rad_ref, sg_ref, sc_ref, wr_ref, br_ref, we_ref, be_ref,
     gates_ref, stats_ref, feat_ref,
     send_rad, recv_rad, full_rad, squeeze, gate,
     rs_send, rs_recv, ag_send, ag_recv, sq_send, sq_recv, gt_send, gt_recv,
@@ -142,7 +139,6 @@
     my_row = lax.axis_index("row")
     my_ch = lax.axis_index("ch")
     chans = stats_ref.shape[-1]
-    units = we_ref.shape[0]
     cells = rows * cols * count_row
     gen_peers = [(off, {"gen": lax.rem(my_gen + off, count_gen)}) for off in range(1, count_gen)]
     side_peers = []
@@ -206,12 +202,12 @@
     for slot in range(1, count_row * count_ch):
         total = total + squeeze[slot]
     row_of = lax.broadcasted_iota(jnp.int32, total.shape, 0)
-    total = total + jnp.where(row_of == gens, vec_ref[2:3, :units], 0.0)
+    total = total + jnp.where(row_of == gens, br_ref[...][None, :], 0.0)
     ex_all = jnp.dot(
         total, we_ref[...], precision=lax.Precision.HIGHEST, preferred_element_type=jnp.float32
     )
     ex_gens = ex_all[:gens]
-    ex_center = ex_all[gens : gens + 1] + vec_ref[1:2]
+    ex_center = ex_all[gens : gens + 1] + be_ref[...][None, :]
     gate[my_gen] = jnp.sum(jnp.abs(ex_gens), axis=0, keepdims=True)
     gt_copies = [
         remote(gate.at[my_gen], gate.at[my_gen], gt_send.at[off], gt_recv.at[off], place)
@@ -250,7 +246,7 @@
     feat_ref[...] = full_rad[:tiles].astype(jnp.float32).reshape(rows, cols, chans)
 
 
-def exchange_call(mesh, radius, sum_gens, sum_center, w_reduce, w_excite, vectors):
+def exchange_call(mesh, radius, sum_gens, sum_center, w_reduce, b_reduce, w_excite, b_excite):
     rows, cols, chans = radius.shape
     gens = sum_gens.shape[0]
     count_gen, count_row, count_ch = mesh["gen"], mesh["row"], mesh["ch"]
@@ -261,7 +257,7 @@
     dma = pltpu.SemaphoreType.DMA
     return pl.pallas_call(
         functools.partial(exchange_kernel, gens, rows, cols, count_gen, count_row, count_ch, per),
-        in_specs=[vmem] * 6,
+        in_specs=[vmem] * 7,
         out_specs=[vmem] * 3,
         out_shape=[
             jax.ShapeDtypeStruct((gens, 1, chans), jnp.float32),
@@ -280,7 +276,7 @@
         compiler_params=pltpu.CompilerParams(
             collective_id=1, has_side_effects=True, vmem_limit_bytes=12 << 20
         ),
-    )(radius, sum_gens, sum_center, w_reduce, w_excite, vectors)
+    )(radius, sum_gens, sum_center, w_reduce, b_reduce, w_excite, b_excite)
 
 
 def final_kernel(block, dwg_ref, gates_ref, dwc_ref, feat_ref, stats_ref, oc_ref, og_ref, ob_ref):
@@ -329,13 +325,11 @@
     taps = w_depth.shape[0]
     c_in, chans = w_expand.shape
     wide = -(-chans // LANES) * LANES
-    bias = b_expand.astype(jnp.bfloat16)
-    rest = (b_expand - bias.astype(jnp.float32)).astype(jnp.bfloat16)
-    mixed = jnp.concatenate([w_expand, bias[None], rest[None]], axis=0)
-    mixed = jnp.pad(mixed, ((0, LANES - c_in - 2), (0, wide - chans))).astype(jnp.float32)
+    mixed = jnp.concatenate([w_expand.astype(jnp.float32), b_expand[None]], axis=0)
+    mixed = jnp.pad(mixed, ((0, LANES - c_in - 1), (0, wide - chans)))
     depth = jnp.pad(w_depth, ((0, 0), (0, 0), (0, wide - chans))).transpose(1, 0, 2)
     merged = (depth[:, :, None, :] * mixed[None, None]).astype(jnp.bfloat16)
-    return merged.reshape(taps, taps * LANES, wide)
+    return merged.reshape(taps * taps * LANES, wide)
 
 
 def halo_kernel(count_row, count_ch, margin, x_ref, out_ref, send_sem, recv_sem, fwd_send, fwd_recv):
@@ -439,19 +433,17 @@
     taps = w_depth.shape[0]
     margin = taps // 2
     weights = merged_weights(w_expand, b_expand, w_depth)
-    ones = jnp.ones((rows, cols, 2), jnp.bfloat16)
+    ones = jnp.ones((rows, cols, 1), jnp.bfloat16)
     center = jnp.concatenate([x_center, ones], axis=-1)
-    center = jnp.pad(center, ((0, 0), (0, cols), (0, LANES - c_in - 2)))
+    center = jnp.pad(center, ((0, 0), (0, cols), (0, LANES - c_in - 1)))
     flat = x_gens.transpose(1, 0, 2, 3).reshape(rows, gens * cols, c_in)
     flat = jnp.concatenate([jnp.pad(flat, ((0, 0), (0, 0), (0, LANES - c_in))), center], axis=1)
     x_rows = halo_call(shape, flat, margin)
-    units = b_reduce.shape[0]
-    vectors = jnp.stack([b_depth, b_excite, jnp.pad(b_reduce, (0, chans - units))])
     dw_gens, dw_center, local_radius, sum_gens, sum_center = conv_call(
-        x_rows, weights, vectors, gens, rows, taps, cols
+        x_rows, weights, b_depth, gens, rows, taps, cols
     )
     gates, stats, feat = exchange_call(
-        shape, local_radius, sum_gens, sum_center, w_reduce.T, w_excite, vectors
+        shape, local_radius, sum_gens, sum_center, w_reduce.T, b_reduce, w_excite, b_excite
     )
     return final_call(dw_gens, gates, dw_center, feat, stats)
 

time: 57.9 us -> 52.2 us (0.902)
  Pallas kernels: 50.3 us -> 45.5 us
  other arithmetic: 3.22 us -> 2.57 us
    pallas_call x1, Pallas kernels: 24.8 us -> 20 us  [conv_call(): pl.pallas_call(functools.partial(conv_kernel, rows, taps, cols, block, ch...]
    another operation x3 -> x0, local copies, waits for them, and re-layouts: 1.47 us -> none  [on_device(): jnp.stack([b_depth, b_excite, jnp.pad(b_reduce, (0, chans - units))])]
    transpose x1, local copies, waits for them, and re-layouts: 0.2 us -> 1.48 us  [on_device(): flat = x_gens.transpose(1, 0, 2, 3).reshape(rows, gens * cols, c_in)]
    convert_element_type x2 -> x1, other arithmetic: 1.68 us -> 0.9 us  [merged_weights(): w_expand.astype(jnp.float32)]
    broadcast_in_dim x2 -> x1, local copies, waits for them, and re-layouts: 0.01 us -> 0.68 us  [merged_weights(): b_expand[None]]
    pad x1 -> x0, local copies, waits for them, and re-layouts: 0.66 us -> none  [on_device(): jnp.pad(b_reduce, (0, chans - units))]
where the time goes in v5:
time: 52.2 us; the launch traced here: 51.9 us
  Pallas kernels  45.5 us (87%)
  local copies, waits for them, and re-layouts  3.04 us (6%)
  other arithmetic  2.57 us (5%)
  between operations  0.77 us (1%)
    pallas_call x1, Pallas kernels, conv_call(): pl.pallas_call(functools.partial(conv_kernel, rows, taps, cols, block, ch...  20 us
    pallas_call x1, Pallas kernels, exchange_call(): pl.pallas_call(functools.partial(exchange_kernel, gens, rows, cols, count...  12.6 us
    pallas_call x1, Pallas kernels, halo_call(): pl.pallas_call(functools.partial(halo_kernel, mesh['row'], mesh['ch'], ma...  10 us
    pallas_call x1, Pallas kernels, final_call(): pl.pallas_call(functools.partial(final_kernel, block), grid=(gens // bloc...  2.92 us
    transpose x1, local copies, waits for them, and re-layouts, on_device(): flat = x_gens.transpose(1, 0, 2, 3).reshape(rows, gens * cols, c_in)  1.48 us

profile of v5, /device:TPU:0, one launch (start us, length us, event | category | flops | bytes accessed | tf_op | source)
XLA Modules:
  0.0 51.9 jit_solution(16674162932651296556)
XLA Ops:
  0.6 0.7 %broadcast_in_dim.2 = f32[1,336]{1,0:T(1,128)S(1)} reshape(f32[336]{0:T(512)} %param.13) | data formatting | bytes 2688 | tf_op jit(solution)/shard_map/broadcast_in_dim | solution.py:328
  1.3 0.8 %pad_bitcast_fusion = f32[5,5,384]{2,0,1:T(8,128)S(1)} fusion(f32[5,5,336]{2,1,0:T(8,128)} %param.14), kind=kLoop, calls=%fused_computation.12 | loop fusion | bytes 72000 | tf_op jit(solution)/shard_map/transpose | solution.py:330
  2.2 0.8 %fusion.4 = bf16[6,48,128]{2,1,0:T(8,128)(2,1)S(1)} fusion(bf16[6,24,112]{2,1,0:T(8,128)(2,1)} %param.10), kind=kLoop, calls=%fused_computation.11 | loop fusion | flops 184320 | bytes 105984 | tf_op jit(solution)/shard_map/jit(_pad)/pad | solution.py:438
  3.0 0.9 %convert_element_type.18 = f32[112,336]{1,0:T(8,128)S(1)} convert(bf16[112,336]{1,0:T(8,128)(2,1)} %param.12) | non-fusion elementwise | flops 37632 | bytes 225792 | tf_op jit(solution)/shard_map/convert_element_type | solution.py:328
  3.9 1.5 %copy.13 = bf16[6,32,24,112]{3,2,1,0:T(8,128)(2,1)S(1)} copy(bf16[6,32,24,112]{3,2,0,1:T(8,128)(2,1)} %bitcast.9) | data formatting | bytes 2064384 | tf_op jit(solution)/shard_map/transpose | solution.py:439
  5.4 0.2 fusion.1.x_ref
  5.6 0.0 copy-start.4
  5.6 10.0 %shard_map.121.x_ref = bf16[10,816,128]{2,1,0:T(8,128)(2,1)S(1)} custom-call(bf16[6,816,128]{2,1,0:T(8,128)(2,1)S(1)} %fusion.1.x_ref), custom_call_target="tpu_custom_call" | custom-call | tf_op jit(solution)/shard_map/pallas_call | solution.py:414
  15.6 0.6 %multiply_convert_fusion = bf16[5,5,128,384]{3,2,1,0:T(8,128)(2,1)S(1)} fusion(f32[128,384]{1,0:T(8,128)S(1)} %select_maximum_fusion, f32[5,5,384]{2,1,0:T(8,128)S(1)} %copy.14), kind=kLoop, calls=%fused_computation | loop fusion | flops 2457600 | bytes 2692608 | tf_op jit(solution)/shard_map/convert_element_type | solution.py:331
  16.3 0.0 copy-done.4
  16.3 0.0 copy-start
  16.3 0.0 copy-start.1
  16.3 0.0 copy-start.2
  16.3 0.0 copy-start.3
  16.3 20.0 %shard_map.122 = (bf16[32,6,24,336]{3,2,1,0:T(8,128)(2,1)S(1)}, f32[6,24,336]{2,1,0:T(8,128)S(1)}, f32[6,24,336]{2,1,0:T(8,128)S(1)}, f32[32,1,336]{2,1,0:T(1,128)S(1)}, f32[1,336]{1,0:T(1,128)S(1)}) custom-call(bf16[10,816,128]{2,1,0:T(8,128)(2,1)S(1)} %shard_map.121.x_ref, bf16[3200,384]{1,0:T(8,128)(2,1)S(1)} %bitcast.6, f32[336]{0:T(512)S(1)} %copy-done.4), custom_call_target="tpu_custom_call" | custom-call | flops 11324620800 | bytes 10485760 | tf_op jit(solution)/shard_map/pallas_call | solution.py:81
  36.4 0.0 copy-done
  36.4 0.0 copy-done.1
  36.4 0.0 copy-done.2
  36.4 0.0 copy-done.3
  36.4 12.6 %shard_map.123 = (f32[32,1,336]{2,1,0:T(1,128)S(1)}, f32[3,336]{1,0:T(4,128)S(1)}, f32[6,24,336]{2,1,0:T(8,128)S(1)}) custom-call(f32[6,24,336]{2,1,0:T(8,128)S(1)} %get-tuple-element.12.rad_ref, f32[32,1,336]{2,1,0:T(1,128)S(1)} %get-tuple-element.13.sg_ref, f32[1,336]{1,0:T(1,128)S(1)} %get-tuple-element.14.sc_ref, f32[28,672]{1,0:T(8,128)S(1)} %bitcast.7, ...), custom_call_target="tpu_custom_call" | custom-call | tf_op jit(solution)/shard_map/pallas_call | solution.py:258
  49.0 2.9 %shard_map.124 = (f32[6,24,336]{2,1,0:T(8,128)}, bf16[32,6,24,336]{3,2,1,0:T(8,128)(2,1)}, f32[6,24,336]{2,1,0:T(8,128)}) custom-call(bf16[32,6,24,336]{3,2,1,0:T(8,128)(2,1)S(1)} %get-tuple-element.11.dwg_ref, f32[32,1,336]{2,1,0:T(1,128)S(1)} %get-tuple-element.15.gates_ref, f32[6,24,336]{2,1,0:T(8,128)S(1)} %get-tuple-element.16.dwc_ref, ...), custom_call_target="tpu_custom_call" | custom-call | tf_op jit(solution)/shard_map/pallas_call | solution.py:302
  (2 shorter events, 0.0 us)
Async XLA Ops:
  5.6 10.7 %copy-start.4 = (f32[336]{0:T(512)S(1)}, f32[336]{0:T(512)}, u32[]{:S(2)}) copy-start(f32[336]{0:T(512)} %bd_ref.1) | copy-start | bytes 4036
  16.3 20.1 %copy-start = (f32[672,28]{0,1:T(8,128)S(1)}, f32[672,28]{0,1:T(8,128)}, u32[]{:S(2)}) copy-start(f32[672,28]{0,1:T(8,128)} %param.16) | copy-start | bytes 225796
  16.3 20.1 %copy-start.1 = (f32[28,336]{1,0:T(8,128)S(1)}, f32[28,336]{1,0:T(8,128)}, u32[]{:S(2)}) copy-start(f32[28,336]{1,0:T(8,128)} %we_ref.1) | copy-start | bytes 112900
  16.3 20.1 %copy-start.2 = (f32[336]{0:T(512)S(1)}, f32[336]{0:T(512)}, u32[]{:S(2)}) copy-start(f32[336]{0:T(512)} %be_ref.1) | copy-start | bytes 4036
  16.3 20.1 %copy-start.3 = (f32[28]{0:T(128)S(1)}, f32[28]{0:T(128)}, u32[]{:S(2)}) copy-start(f32[28]{0:T(128)} %br_ref.1) | copy-start | bytes 340

commit v6 on v5

--- a/solution.py
+++ b/solution.py
@@ -296,7 +296,7 @@
 
 def final_call(dw_gens, gates, dw_center, feat, stats):
     gens, rows, cols, chans = dw_gens.shape
-    block = 8
+    block = 4
     whole = pl.BlockSpec((rows, cols, chans), lambda i: (0, 0, 0))
     big = pl.BlockSpec((block, rows, cols, chans), lambda i: (i, 0, 0, 0))
     return pl.pallas_call(

time: 52.2 us -> 53.4 us (1.023)
  Pallas kernels: 45.5 us -> 46.7 us
    pallas_call x1, Pallas kernels: 2.92 us -> 4.03 us  [final_call(): pl.pallas_call(functools.partial(final_kernel, block), grid=(gens // bloc...]
where the time goes in v6:
time: 53.4 us; the launch traced here: 53 us
  Pallas kernels  46.7 us (87%)
  local copies, waits for them, and re-layouts  3.04 us (6%)
  other arithmetic  2.57 us (5%)
  between operations  0.77 us (1%)
    pallas_call x1, Pallas kernels, conv_call(): pl.pallas_call(functools.partial(conv_kernel, rows, taps, cols, block, ch...  20 us
    pallas_call x1, Pallas kernels, exchange_call(): pl.pallas_call(functools.partial(exchange_kernel, gens, rows, cols, count...  12.6 us
    pallas_call x1, Pallas kernels, halo_call(): pl.pallas_call(functools.partial(halo_kernel, mesh['row'], mesh['ch'], ma...  10 us
    pallas_call x1, Pallas kernels, final_call(): pl.pallas_call(functools.partial(final_kernel, block), grid=(gens // bloc...  4.03 us
    transpose x1, local copies, waits for them, and re-layouts, on_device(): flat = x_gens.transpose(1, 0, 2, 3).reshape(rows, gens * cols, c_in)  1.48 us

profile of v6, /device:TPU:0, one launch (start us, length us, event | category | flops | bytes accessed | tf_op | source)
XLA Modules:
  0.0 53.0 jit_solution(8875418055818891344)
XLA Ops:
  0.6 0.7 %broadcast_in_dim.2 = f32[1,336]{1,0:T(1,128)S(1)} reshape(f32[336]{0:T(512)} %param.13) | data formatting | bytes 2688 | tf_op jit(solution)/shard_map/broadcast_in_dim | solution.py:328
  1.3 0.8 %pad_bitcast_fusion = f32[5,5,384]{2,0,1:T(8,128)S(1)} fusion(f32[5,5,336]{2,1,0:T(8,128)} %param.14), kind=kLoop, calls=%fused_computation.12 | loop fusion | bytes 72000 | tf_op jit(solution)/shard_map/transpose | solution.py:330
  2.2 0.8 %fusion.4 = bf16[6,48,128]{2,1,0:T(8,128)(2,1)S(1)} fusion(bf16[6,24,112]{2,1,0:T(8,128)(2,1)} %param.10), kind=kLoop, calls=%fused_computation.11 | loop fusion | flops 184320 | bytes 105984 | tf_op jit(solution)/shard_map/jit(_pad)/pad | solution.py:438
  3.0 0.9 %convert_element_type.18 = f32[112,336]{1,0:T(8,128)S(1)} convert(bf16[112,336]{1,0:T(8,128)(2,1)} %param.12) | non-fusion elementwise | flops 37632 | bytes 225792 | tf_op jit(solution)/shard_map/convert_element_type | solution.py:328
  3.9 1.5 %copy.13 = bf16[6,32,24,112]{3,2,1,0:T(8,128)(2,1)S(1)} copy(bf16[6,32,24,112]{3,2,0,1:T(8,128)(2,1)} %bitcast.9) | data formatting | bytes 2064384 | tf_op jit(solution)/shard_map/transpose | solution.py:439
  5.4 0.2 fusion.1.x_ref
  5.6 0.0 copy-start.4
  5.6 10.0 %shard_map.121.x_ref = bf16[10,816,128]{2,1,0:T(8,128)(2,1)S(1)} custom-call(bf16[6,816,128]{2,1,0:T(8,128)(2,1)S(1)} %fusion.1.x_ref), custom_call_target="tpu_custom_call" | custom-call | tf_op jit(solution)/shard_map/pallas_call | solution.py:414
  15.6 0.6 %multiply_convert_fusion = bf16[5,5,128,384]{3,2,1,0:T(8,128)(2,1)S(1)} fusion(f32[128,384]{1,0:T(8,128)S(1)} %select_maximum_fusion, f32[5,5,384]{2,1,0:T(8,128)S(1)} %copy.14), kind=kLoop, calls=%fused_computation | loop fusion | flops 2457600 | bytes 2692608 | tf_op jit(solution)/shard_map/convert_element_type | solution.py:331
  16.3 0.0 copy-done.4
  16.3 0.0 copy-start
  16.3 0.0 copy-start.1
  16.3 0.0 copy-start.2
  16.3 0.0 copy-start.3
  16.3 20.0 %shard_map.122 = (bf16[32,6,24,336]{3,2,1,0:T(8,128)(2,1)S(1)}, f32[6,24,336]{2,1,0:T(8,128)S(1)}, f32[6,24,336]{2,1,0:T(8,128)S(1)}, f32[32,1,336]{2,1,0:T(1,128)S(1)}, f32[1,336]{1,0:T(1,128)S(1)}) custom-call(bf16[10,816,128]{2,1,0:T(8,128)(2,1)S(1)} %shard_map.121.x_ref, bf16[3200,384]{1,0:T(8,128)(2,1)S(1)} %bitcast.6, f32[336]{0:T(512)S(1)} %copy-done.4), custom_call_target="tpu_custom_call" | custom-call | flops 11324620800 | bytes 10485760 | tf_op jit(solution)/shard_map/pallas_call | solution.py:81
  36.4 0.0 copy-done
  36.4 0.0 copy-done.1
  36.4 0.0 copy-done.2
  36.4 0.0 copy-done.3
  36.4 12.6 %shard_map.123 = (f32[32,1,336]{2,1,0:T(1,128)S(1)}, f32[3,336]{1,0:T(4,128)S(1)}, f32[6,24,336]{2,1,0:T(8,128)S(1)}) custom-call(f32[6,24,336]{2,1,0:T(8,128)S(1)} %get-tuple-element.12.rad_ref, f32[32,1,336]{2,1,0:T(1,128)S(1)} %get-tuple-element.13.sg_ref, f32[1,336]{1,0:T(1,128)S(1)} %get-tuple-element.14.sc_ref, f32[28,672]{1,0:T(8,128)S(1)} %bitcast.7, ...), custom_call_target="tpu_custom_call" | custom-call | tf_op jit(solution)/shard_map/pallas_call | solution.py:258
  49.0 4.0 %shard_map.124 = (f32[6,24,336]{2,1,0:T(8,128)}, bf16[32,6,24,336]{3,2,1,0:T(8,128)(2,1)}, f32[6,24,336]{2,1,0:T(8,128)}) custom-call(bf16[32,6,24,336]{3,2,1,0:T(8,128)(2,1)S(1)} %get-tuple-element.11.dwg_ref, f32[32,1,336]{2,1,0:T(1,128)S(1)} %get-tuple-element.15.gates_ref, f32[6,24,336]{2,1,0:T(8,128)S(1)} %get-tuple-element.16.dwc_ref, ...), custom_call_target="tpu_custom_call" | custom-call | tf_op jit(solution)/shard_map/pallas_call | solution.py:302
  (2 shorter events, 0.0 us)
Async XLA Ops:
  5.6 10.7 %copy-start.4 = (f32[336]{0:T(512)S(1)}, f32[336]{0:T(512)}, u32[]{:S(2)}) copy-start(f32[336]{0:T(512)} %bd_ref.1) | copy-start | bytes 4036
  16.3 20.1 %copy-start = (f32[672,28]{0,1:T(8,128)S(1)}, f32[672,28]{0,1:T(8,128)}, u32[]{:S(2)}) copy-start(f32[672,28]{0,1:T(8,128)} %param.16) | copy-start | bytes 225796
  16.3 20.1 %copy-start.1 = (f32[28,336]{1,0:T(8,128)S(1)}, f32[28,336]{1,0:T(8,128)}, u32[]{:S(2)}) copy-start(f32[28,336]{1,0:T(8,128)} %we_ref.1) | copy-start | bytes 112900
  16.3 20.1 %copy-start.2 = (f32[336]{0:T(512)S(1)}, f32[336]{0:T(512)}, u32[]{:S(2)}) copy-start(f32[336]{0:T(512)} %be_ref.1) | copy-start | bytes 4036
  16.3 20.1 %copy-start.3 = (f32[28]{0:T(128)S(1)}, f32[28]{0:T(128)}, u32[]{:S(2)}) copy-start(f32[28]{0:T(128)} %br_ref.1) | copy-start | bytes 340
